TPU v7x, 32 devices: a whole 2x2x4 slice. The times are simulated.
32 devices in a mesh: row: 4 (over z), col: 8 (over y, x, core).
Axes of the slice: x: 2, y: 2, z: 4, core: 2. Of those that a mesh axis runs over, the one named last changes fastest.
Arguments:
- strain: bfloat16 [256, 33280], P(('row', 'col')), may hold values from -6 to 6
- file_channels: int32 [256], P(('row', 'col')), may hold values from 0 to 127, as said below
- file_counts: int32 [32], P(('row', 'col')), may hold values from 0 to 8, as said below
- window_start: int32 [32], P(('row', 'col')), may hold values from 0 to 512
Outputs:
- correlations: bfloat16 [128, 128, 1024], P('row', 'col')
Inputs may be any that keep to these rules, and one draw needn't show every extreme that they name: `file_channels`: the first file_counts[d] slots of file d are live. The live slots of the 4 files with one col index hold, each exactly once, the channels g whose owner ((g // 4) // 8, (g // 4) % 8) has that col index; dead slots hold arbitrary channel numbers. One file holds at most 2 channels of one owner, and exactly 2 for some file and owner in every group of files with one col index. `file_counts`: in every group of files with one col index some file has all 8 slots live.
All inputs are finite; a program needn't handle non-finite values.
Results may differ from a plain program's by a relative error of at most 0.0076.
Values may be sent and summed in bfloat16 or wider, within the bound.
A program may use at most 128 MiB of HBM per device.

v0:
```python
import math

import jax
import jax.numpy as jnp
from jax import lax
from jax.sharding import PartitionSpec as P

NF = 2048
NT = 4096
LAGS = 1024
SEGS = 8
CH_DEV = 4
CAP = 2
SMOOTH = 32
EDGE = 128


def dft_block(first_freq, freq_count, length):
    sample_index = jnp.arange(length, dtype=jnp.int32)[:, None]
    freq_index = first_freq + jnp.arange(freq_count, dtype=jnp.int32)[None, :]
    phases = jnp.mod(sample_index * freq_index, length).astype(jnp.float32) * (
        2.0 * math.pi / length
    )
    return jnp.concatenate([jnp.cos(phases), -jnp.sin(phases)], axis=1).astype(jnp.bfloat16)


def lag_table():
    freq_index = jnp.arange(NF, dtype=jnp.int32)[:, None]
    lag_index = jnp.arange(LAGS, dtype=jnp.int32)[None, :] - LAGS // 2
    phases = jnp.mod(freq_index * lag_index, NT).astype(jnp.float32) * (2.0 * math.pi / NT)
    return jnp.concatenate([jnp.cos(phases), -jnp.sin(phases)], axis=0).astype(jnp.bfloat16)


def band_taper(freq_count):
    freq_index = jnp.arange(freq_count, dtype=jnp.float32)
    distance = jnp.minimum(freq_index + 0.5, freq_count - freq_index - 0.5)
    rising = jnp.minimum(distance / EDGE, 1.0)
    return jnp.sin(0.5 * math.pi * rising) ** 2


def whiten(real_part, imag_part):
    powers = real_part * real_part + imag_part * imag_part
    padded = jnp.pad(powers, ((0, 0), (SMOOTH + 1, SMOOTH)))
    running = jnp.cumsum(padded, axis=1)
    window_sum = running[:, 2 * SMOOTH + 1 :] - running[:, : powers.shape[1]]
    scaling = band_taper(powers.shape[1])[None, :] / jnp.sqrt(window_sum / (2 * SMOOTH + 1) + 1e-06)
    return (real_part * scaling, imag_part * scaling)


def spectra_of(traces):
    channels = traces.shape[0]
    segment_rows = traces.reshape(channels * SEGS, NT)
    block_width = min(256, NF)
    block_count = NF // block_width

    def spectra_one_block(block_index):
        table = dft_block(block_index * block_width, block_width, NT)
        return jnp.dot(segment_rows, table, preferred_element_type=jnp.float32)

    pieces = lax.map(spectra_one_block, jnp.arange(block_count, dtype=jnp.int32))
    pieces = pieces.reshape(block_count, channels * SEGS, 2, block_width)
    real_part = jnp.transpose(pieces[:, :, 0], (1, 0, 2)).reshape(channels * SEGS, NF)
    imag_part = jnp.transpose(pieces[:, :, 1], (1, 0, 2)).reshape(channels * SEGS, NF)
    real_part, imag_part = whiten(real_part, imag_part)
    stacked = jnp.stack(
        [real_part.reshape(channels, SEGS, NF), imag_part.reshape(channels, SEGS, NF)], axis=1
    )
    return stacked.astype(jnp.bfloat16)


def correlate(row_spectra, row_ids, col_spectra, col_ids, inverse):
    flipped = jnp.concatenate([-col_spectra[:, 1:2], col_spectra[:, 0:1]], axis=1)
    row_total = row_spectra.shape[0]
    col_total = col_spectra.shape[0]
    block_cols = 8
    norm_scale = 1.0 / math.sqrt(SEGS * NF)

    def correlate_one_block(block_index):
        first_col = block_index * block_cols
        own_cols = lax.dynamic_slice_in_dim(col_spectra, first_col, block_cols, 0)
        turned = lax.dynamic_slice_in_dim(flipped, first_col, block_cols, 0)
        real_cross = jnp.einsum(
            "icsf,jcsf->ijf", row_spectra, own_cols, preferred_element_type=jnp.float32
        )
        imag_cross = jnp.einsum(
            "icsf,jcsf->ijf", row_spectra, turned, preferred_element_type=jnp.float32
        )
        cross = jnp.concatenate([real_cross, imag_cross], axis=2).astype(jnp.bfloat16)
        lagged = jnp.dot(
            cross.reshape(row_total * block_cols, 2 * NF),
            inverse,
            preferred_element_type=jnp.float32,
        )
        block_ids = lax.dynamic_slice_in_dim(col_ids, first_col, block_cols, 0)
        keep_pair = (row_ids[:, None] != block_ids[None, :]).astype(jnp.float32)
        lagged = lagged.reshape(row_total, block_cols, LAGS)
        return (lagged * (keep_pair[:, :, None] * norm_scale)).astype(jnp.bfloat16)

    results = lax.map(correlate_one_block, jnp.arange(col_total // block_cols, dtype=jnp.int32))
    return jnp.transpose(results, (1, 0, 2, 3)).reshape(row_total, col_total, LAGS)


def local(strain, file_channels, file_counts, window_start):
    row_count = lax.axis_size("row")
    col_count = lax.axis_size("col")
    my_row = lax.axis_index("row")
    my_col = lax.axis_index("col")
    slot_total = strain.shape[0]
    window = lax.dynamic_slice_in_dim(strain, window_start[0], SEGS * NT, 1)
    slot_index = jnp.arange(slot_total, dtype=jnp.int32)
    live_slot = slot_index < file_counts[0]
    owner_row = file_channels // CH_DEV // col_count
    local_slot = file_channels % CH_DEV
    same_owner = (owner_row[:, None] == owner_row[None, :]) & live_slot[None, :]
    earlier = slot_index[None, :] < slot_index[:, None]
    position = jnp.sum((same_owner & earlier).astype(jnp.int32), axis=1)
    target = owner_row * CAP + position
    routing = (
        jnp.arange(row_count * CAP, dtype=jnp.int32)[:, None] == target[None, :]
    ) & live_slot[None, :]
    outgoing = jnp.dot(
        routing.astype(jnp.bfloat16), window, preferred_element_type=jnp.float32
    ).astype(jnp.bfloat16)
    labels = jnp.sum(jnp.where(routing, local_slot[None, :] + 1, 0), axis=1) - 1
    arrived, arrived_labels = (
        lax.all_to_all(
            outgoing.reshape(row_count, CAP, SEGS * NT),
            "row",
            split_axis=0,
            concat_axis=0,
            tiled=True,
        ),
        lax.all_to_all(
            labels.astype(jnp.bfloat16).reshape(row_count, CAP),
            "row",
            split_axis=0,
            concat_axis=0,
            tiled=True,
        ),
    )
    arrived = arrived.reshape(row_count * CAP, SEGS * NT)
    wanted = jnp.arange(CH_DEV, dtype=jnp.float32)
    picking = (arrived_labels.reshape(-1).astype(jnp.float32)[None, :] == wanted[:, None]).astype(
        jnp.bfloat16
    )
    traces = jnp.dot(picking, arrived, preferred_element_type=jnp.float32).astype(jnp.bfloat16)
    own_spectra = spectra_of(traces)
    col_spectra = lax.all_gather(own_spectra, "row", axis=0, tiled=True)
    col_local = jnp.arange(col_spectra.shape[0], dtype=jnp.int32)
    col_ids = (col_local // CH_DEV * col_count + my_col) * CH_DEV + col_local % CH_DEV
    row_base = my_row * col_count * CH_DEV
    inverse = lag_table()
    row_spectra = lax.all_gather(own_spectra, "col", axis=0, tiled=True)
    row_ids = row_base + jnp.arange(row_spectra.shape[0], dtype=jnp.int32)
    return correlate(row_spectra, row_ids, col_spectra, col_ids, inverse)


def solution(mesh):
    placed = (P(("row", "col"), None), P(("row", "col")), P(("row", "col")), P(("row", "col")))
    return jax.shard_map(
        local, mesh=mesh, in_specs=placed, out_specs=P("row", "col", None), check_vma=False
    )
```

profile of v0, /device:TPU:0, one launch (start us, length us, event | category | flops | bytes accessed | tf_op | source)
XLA Modules:
  0.0 389.5 jit_solution(460141560468628709)
XLA Ops:
  6.5 0.7 fusion.76
  8.9 6.3 %all-to-all-start = ((bf16[4,1,2]{2,1,0:T(2,128)(2,1)}), bf16[4,1,2]{2,1,0:T(2,128)(2,1)S(1)}, u32[]{:S(2)}, u32[]{:S(2)}) async-start(bf16[4,1,2]{2,1,0:T(2,128)(2,1)} %convert_element_type.72), calls=%async_computation | async-start | bytes 4096 | tf_op jit(solution)/shard_map/all_to_all | solution.py:133
  16.3 1.1 reshape.133
  17.4 3.3 all-to-all-done
  20.7 3.5 all-to-all-start.1
  24.4 13.2 %all-to-all-done.1 = bf16[4,2,32768]{2,1,0:T(2,128)(2,1)S(1)} async-done(((bf16[4,2,32768]{2,1,0:T(2,128)(2,1)}), bf16[4,2,32768]{2,1,0:T(2,128)(2,1)S(1)}, u32[]{:S(2)}, u32[]{:S(2)}) %all-to-all-start.1) | async-done | bytes 524320 | tf_op jit(solution)/shard_map/all_to_all | solution.py:126
  38.4 152.4 %while.23 = (s32[]{:T(128)}, f32[8,32,512]{2,1,0:T(8,128)S(1)}, s32[8]{0:T(128)S(1)}, bf16[32,4096]{1,0:T(8,128)(2,1)S(1)}, s32[]{:T(128)}, /*index=5*/s32[1]{0:T(128)}) while((s32[]{:T(128)}, f32[8,32,512]{2,1,0:T(8,128)S(1)}, s32[8]{0:T(128)S(1)}, bf16[32,4096]{1,0:T(8,128)(2,1)S(1)}, s32[]{:T(128)}, /*index=5*/s32[1]{0:T(128)}) %tuple.56), condition=%wide.region_3.4_spmd, body=%wide.region_2.3_spmd.sunk | while | flops 160432384 | bytes 8718437 | solution.py:60
  39.6 17.0 %cosine_convert_fusion.3 = (bf16[4096,256]{1,0:T(8,128)(2,1)S(1)}, bf16[4096,256]{1,0:T(8,128)(2,1)S(1)}) fusion(s32[256]{0:T(256)S(1)} %iota_add_fusion.6), kind=kLoop, calls=%fused_computation.12.clone.1 | loop fusion | flops 17825792 | bytes 4195328 | tf_op jit(solution)/shard_map/convert.4
  56.6 0.8 fusion.100
  58.7 17.0 %cosine_convert_fusion.3 = (bf16[4096,256]{1,0:T(8,128)(2,1)S(1)}, bf16[4096,256]{1,0:T(8,128)(2,1)S(1)}) fusion(s32[256]{0:T(256)S(1)} %iota_add_fusion.6), kind=kLoop, calls=%fused_computation.12.clone.1 | loop fusion | flops 17825792 | bytes 4195328 | tf_op jit(solution)/shard_map/convert.4
  75.6 0.8 fusion.100
  77.7 17.0 %cosine_convert_fusion.3 = (bf16[4096,256]{1,0:T(8,128)(2,1)S(1)}, bf16[4096,256]{1,0:T(8,128)(2,1)S(1)}) fusion(s32[256]{0:T(256)S(1)} %iota_add_fusion.6), kind=kLoop, calls=%fused_computation.12.clone.1 | loop fusion | flops 17825792 | bytes 4195328 | tf_op jit(solution)/shard_map/convert.4
  94.7 0.8 fusion.100
  96.8 17.0 %cosine_convert_fusion.3 = (bf16[4096,256]{1,0:T(8,128)(2,1)S(1)}, bf16[4096,256]{1,0:T(8,128)(2,1)S(1)}) fusion(s32[256]{0:T(256)S(1)} %iota_add_fusion.6), kind=kLoop, calls=%fused_computation.12.clone.1 | loop fusion | flops 17825792 | bytes 4195328 | tf_op jit(solution)/shard_map/convert.4
  113.8 0.8 fusion.100
  115.8 17.0 %cosine_convert_fusion.3 = (bf16[4096,256]{1,0:T(8,128)(2,1)S(1)}, bf16[4096,256]{1,0:T(8,128)(2,1)S(1)}) fusion(s32[256]{0:T(256)S(1)} %iota_add_fusion.6), kind=kLoop, calls=%fused_computation.12.clone.1 | loop fusion | flops 17825792 | bytes 4195328 | tf_op jit(solution)/shard_map/convert.4
  132.8 0.8 fusion.100
  134.9 17.0 %cosine_convert_fusion.3 = (bf16[4096,256]{1,0:T(8,128)(2,1)S(1)}, bf16[4096,256]{1,0:T(8,128)(2,1)S(1)}) fusion(s32[256]{0:T(256)S(1)} %iota_add_fusion.6), kind=kLoop, calls=%fused_computation.12.clone.1 | loop fusion | flops 17825792 | bytes 4195328 | tf_op jit(solution)/shard_map/convert.4
  151.9 0.8 fusion.100
  153.9 17.0 %cosine_convert_fusion.3 = (bf16[4096,256]{1,0:T(8,128)(2,1)S(1)}, bf16[4096,256]{1,0:T(8,128)(2,1)S(1)}) fusion(s32[256]{0:T(256)S(1)} %iota_add_fusion.6), kind=kLoop, calls=%fused_computation.12.clone.1 | loop fusion | flops 17825792 | bytes 4195328 | tf_op jit(solution)/shard_map/convert.4
  170.9 0.8 fusion.100
  173.0 17.0 %cosine_convert_fusion.3 = (bf16[4096,256]{1,0:T(8,128)(2,1)S(1)}, bf16[4096,256]{1,0:T(8,128)(2,1)S(1)}) fusion(s32[256]{0:T(256)S(1)} %iota_add_fusion.6), kind=kLoop, calls=%fused_computation.12.clone.1 | loop fusion | flops 17825792 | bytes 4195328 | tf_op jit(solution)/shard_map/convert.4
  190.0 0.8 fusion.100
  192.4 9.2 %reduce-window.6 = f32[32,17,128]{2,1,0:T(8,128)S(1)} reduce-window(f32[32,17,128]{2,1,0:T(8,128)S(1)} %reshape.139, f32[]{:T(128)} %constant.162.clone.1), window={size=1x1x128 pad=0_0x0_0x127_0}, to_apply=%region_4.5 | reduce-window | flops 8843264 | bytes 557060 | tf_op jit(solution)/shard_map/reduce-window
  204.2 35.0 %cosine_convert_fusion.1 = (bf16[2048,1024]{1,0:T(8,128)(2,1)}, bf16[2048,1024]{1,0:T(8,128)(2,1)}) fusion(s32[1024]{0:T(1024)S(1)} %iota_add_fusion.3), kind=kLoop, calls=%fused_computation.48 | loop fusion | flops 35651584 | bytes 8392704 | tf_op jit(solution)/shard_map/convert.7
  239.2 7.7 %pad_maximum_fusion = bf16[4096,1024]{1,0:T(8,128)(2,1)} fusion(bf16[2048,1024]{1,0:T(8,128)(2,1)} %get-tuple-element.193, bf16[2048,1024]{1,0:T(8,128)(2,1)} %get-tuple-element.192), kind=kLoop, calls=%fused_computation.46 | loop fusion | flops 16777216 | bytes 16777216 | tf_op jit(solution)/shard_map/concatenate | solution.py:31
  246.9 1.3 slice_negate_fusion
  248.2 1.1 pad_maximum_fusion.1
  249.3 10.4 %all-gather.5.cloned.1.call-done = bf16[32,2,8,2048]{3,2,1,0:T(8,128)(2,1)} async-done(((bf16[4,2,8,2048]{3,2,1,0:T(8,128)(2,1)}), bf16[32,2,8,2048]{3,2,1,0:T(8,128)(2,1)}) %all-gather.5.cloned.1.call-update) | async-done | bytes 2097168 | tf_op jit(solution)/shard_map/all_gather | solution.py:153
  259.7 12.8 %copy.50 = bf16[32,2,8,2048]{0,2,1,3:T(8,128)(2,1)} copy(bf16[32,2,8,2048]{3,2,1,0:T(8,128)(2,1)} %all-gather.5.cloned.1.call-done) | data formatting | bytes 4194304
  272.5 107.8 %while.24 = (s32[]{:T(128)}, bf16[2,32,8,1024]{3,2,1,0:T(8,128)(2,1)}, s32[2]{0:T(128)S(1)}, bf16[16,2,8,2048]{3,2,1,0:T(8,128)(2,1)}, bf16[32,2,8,2048]{0,2,1,3...) while((s32[]{:T(128)}, ...), condition=%wide.region_7.8_spmd.clone, body=%wide.region_6.7_spmd.clone.sunk | while | flops 2186805760 | bytes 26741796 | solution.py:99
  273.7 1.3 constant_dynamic-slice_fusion.3
  274.9 8.5 %copy.70 = bf16[8,2,8,2048]{2,0,1,3:T(8,128)(2,1)} copy(bf16[8,2,8,2048]{3,2,1,0:T(8,128)(2,1)S(1)} %get-tuple-element.282) | data formatting | bytes 1048576 | tf_op jit(solution)/shard_map/while/body/eval_jaxpr/dynamic_slice | solution.py:81
  283.5 8.6 %fusion.107 = bf16[32,8,2048]{0,1,2:T(8,128)(2,1)} fusion(bf16[8,2,8,2048]{2,0,1,3:T(8,128)(2,1)} %copy.70, bf16[32,2,8,2048]{0,2,1,3:T(8,128)(2,1)} %get-tuple-element.332), kind=kOutput, calls=%fused_computation.25.clone.1 | convolution fusion | flops 17301504 | bytes 3670016 | tf_op jit(solution)/shard_map/while/body/eval_jaxpr/icsf,jcsf->ijf/dot_general | solution.py:85
  292.1 5.2 %copy.71 = bf16[32,8,2048]{2,1,0:T(8,128)(2,1)S(1)} copy(bf16[32,8,2048]{0,1,2:T(8,128)(2,1)} %fusion.107) | data formatting | bytes 2097152 | tf_op jit(solution)/shard_map/while/body/eval_jaxpr/icsf,jcsf->ijf/transpose | solution.py:85
  297.3 8.5 %copy.72 = bf16[8,2,8,2048]{2,0,1,3:T(8,128)(2,1)} copy(bf16[8,2,8,2048]{3,2,1,0:T(8,128)(2,1)S(1)} %get-tuple-element.283) | data formatting | bytes 1048576 | tf_op jit(solution)/shard_map/while/body/eval_jaxpr/dynamic_slice | solution.py:80
  305.8 8.6 %fusion.108 = bf16[32,8,2048]{0,1,2:T(8,128)(2,1)} fusion(bf16[8,2,8,2048]{2,0,1,3:T(8,128)(2,1)} %copy.72, bf16[32,2,8,2048]{0,2,1,3:T(8,128)(2,1)} %get-tuple-element.332), kind=kOutput, calls=%fused_computation.24.clone.1 | convolution fusion | flops 17301504 | bytes 3670016 | tf_op jit(solution)/shard_map/while/body/eval_jaxpr/icsf,jcsf->ijf/dot_general | solution.py:82
  314.4 5.2 %copy.73 = bf16[32,8,2048]{2,1,0:T(8,128)(2,1)S(1)} copy(bf16[32,8,2048]{0,1,2:T(8,128)(2,1)} %fusion.108) | data formatting | bytes 2097152 | tf_op jit(solution)/shard_map/while/body/eval_jaxpr/icsf,jcsf->ijf/transpose | solution.py:82
  319.8 6.6 %fusion.109 = bf16[2,32,8,1024]{3,2,1,0:T(8,128)(2,1)} fusion(bf16[2,32,8,1024]{3,2,1,0:T(8,128)(2,1)} %get-tuple-element.316, s32[]{:T(128)} %get-tuple-element.315, bf16[4096,1024]{1,0:T(8,128)(2,1)} %get-tuple-element.334, bf16[32,8,2048]{2,1,0:T(8,128)(2,1)S(1)} %copy.71, bf16[32,8,2048]{2,1,0:T(8,128)(2,1)S(1)} %copy.73, ...), kind=kOutput, calls=%fused_computation.32.clone.1 | convolution fusion | flops 2152202240 | bytes 11011584 | tf_op jit(solution)/shard_map/while/body/eval_jaxpr/dot_general | solution.py:89
  327.6 1.3 constant_dynamic-slice_fusion.3
  328.8 8.5 %copy.70 = bf16[8,2,8,2048]{2,0,1,3:T(8,128)(2,1)} copy(bf16[8,2,8,2048]{3,2,1,0:T(8,128)(2,1)S(1)} %get-tuple-element.282) | data formatting | bytes 1048576 | tf_op jit(solution)/shard_map/while/body/eval_jaxpr/dynamic_slice | solution.py:81
  337.3 8.6 %fusion.107 = bf16[32,8,2048]{0,1,2:T(8,128)(2,1)} fusion(bf16[8,2,8,2048]{2,0,1,3:T(8,128)(2,1)} %copy.70, bf16[32,2,8,2048]{0,2,1,3:T(8,128)(2,1)} %get-tuple-element.332), kind=kOutput, calls=%fused_computation.25.clone.1 | convolution fusion | flops 17301504 | bytes 3670016 | tf_op jit(solution)/shard_map/while/body/eval_jaxpr/icsf,jcsf->ijf/dot_general | solution.py:85
  345.9 5.2 %copy.71 = bf16[32,8,2048]{2,1,0:T(8,128)(2,1)S(1)} copy(bf16[32,8,2048]{0,1,2:T(8,128)(2,1)} %fusion.107) | data formatting | bytes 2097152 | tf_op jit(solution)/shard_map/while/body/eval_jaxpr/icsf,jcsf->ijf/transpose | solution.py:85
  351.2 8.5 %copy.72 = bf16[8,2,8,2048]{2,0,1,3:T(8,128)(2,1)} copy(bf16[8,2,8,2048]{3,2,1,0:T(8,128)(2,1)S(1)} %get-tuple-element.283) | data formatting | bytes 1048576 | tf_op jit(solution)/shard_map/while/body/eval_jaxpr/dynamic_slice | solution.py:80
  359.7 8.6 %fusion.108 = bf16[32,8,2048]{0,1,2:T(8,128)(2,1)} fusion(bf16[8,2,8,2048]{2,0,1,3:T(8,128)(2,1)} %copy.72, bf16[32,2,8,2048]{0,2,1,3:T(8,128)(2,1)} %get-tuple-element.332), kind=kOutput, calls=%fused_computation.24.clone.1 | convolution fusion | flops 17301504 | bytes 3670016 | tf_op jit(solution)/shard_map/while/body/eval_jaxpr/icsf,jcsf->ijf/dot_general | solution.py:82
  368.3 5.2 %copy.73 = bf16[32,8,2048]{2,1,0:T(8,128)(2,1)S(1)} copy(bf16[32,8,2048]{0,1,2:T(8,128)(2,1)} %fusion.108) | data formatting | bytes 2097152 | tf_op jit(solution)/shard_map/while/body/eval_jaxpr/icsf,jcsf->ijf/transpose | solution.py:82
  373.7 6.6 %fusion.109 = bf16[2,32,8,1024]{3,2,1,0:T(8,128)(2,1)} fusion(bf16[2,32,8,1024]{3,2,1,0:T(8,128)(2,1)} %get-tuple-element.316, s32[]{:T(128)} %get-tuple-element.315, bf16[4096,1024]{1,0:T(8,128)(2,1)} %get-tuple-element.334, bf16[32,8,2048]{2,1,0:T(8,128)(2,1)S(1)} %copy.71, bf16[32,8,2048]{2,1,0:T(8,128)(2,1)S(1)} %copy.73, ...), kind=kOutput, calls=%fused_computation.32.clone.1 | convolution fusion | flops 2152202240 | bytes 11011584 | tf_op jit(solution)/shard_map/while/body/eval_jaxpr/dot_general | solution.py:89
  380.3 2.3 copy_bitcast_fusion
  (68 shorter events, 12.6 us)
Async XLA Ops:
  6.5 9.4 %copy-start = (bf16[8,33280]{1,0:T(8,128)(2,1)S(1)}, bf16[8,33280]{1,0:T(8,128)(2,1)}, u32[]{:S(2)}) copy-start(bf16[8,33280]{1,0:T(8,128)(2,1)} %param.8) | copy-start | bytes 1597444
  8.9 11.8 %all-to-all-start = ((bf16[4,1,2]{2,1,0:T(2,128)(2,1)}), bf16[4,1,2]{2,1,0:T(2,128)(2,1)S(1)}, u32[]{:S(2)}, u32[]{:S(2)}) async-start(bf16[4,1,2]{2,1,0:T(2,128)(2,1)} %convert_element_type.72), calls=%async_computation | async-start | bytes 4096 | tf_op jit(solution)/shard_map/all_to_all | solution.py:133
  20.7 16.9 %all-to-all-start.1 = ((bf16[4,2,32768]{2,1,0:T(2,128)(2,1)}), bf16[4,2,32768]{2,1,0:T(2,128)(2,1)S(1)}, u32[]{:S(2)}, u32[]{:S(2)}) async-start(bf16[4,2,32768]{2,1,0:T(2,128)(2,1)} %reshape.133), calls=%async_computation.1 | async-start | bytes 1048576 | tf_op jit(solution)/shard_map/all_to_all | solution.py:126
  24.2 222.7 %all-gather.3.cloned.1.call-start = ((), (), s32[]{:S(2)}) async-start(), calls=%async_computation.2 | async-start | bytes 1310720 | tf_op jit(solution)/shard_map/all_gather | solution.py:148
  203.4 56.3 %all-gather.5.cloned.1.call-start = ((), (), s32[]{:S(2)}) async-start(), calls=%async_computation.3 | async-start | bytes 2359296 | tf_op jit(solution)/shard_map/all_gather | solution.py:153
  380.3 2.4 copy-start.1
Sparse Core Ops, SparseCore 0:
  203.5 27.0 all-gather.2
  232.5 27.1 all-gather.4
where the time goes:
time: 390 us; the launch traced here: 389 us
  other arithmetic  193 us (49%)
  local copies, waits for them, and re-layouts  83.1 us (21%)
  matrix products  54.7 us (14%)
  waiting for transfers between devices  27.6 us (7%)
  between operations  14.9 us (4%)
  starting transfers between devices  9.9 us (3%)
  loops' own time  6.55 us (2%)
    another operation x12, other arithmetic  180 us
    dynamic_slice x4, local copies, waits for them, and re-layouts, correlate_one_block(): turned = lax.dynamic_slice_in_dim(flipped, first_col, block_cols, 0)  19.6 us
    dot_general x2, matrix products, correlate_one_block(): jnp.einsum('icsf,jcsf->ijf', row_spectra, turned, preferred_element_type=...  17.2 us
    dot_general x2, matrix products, correlate_one_block(): jnp.einsum('icsf,jcsf->ijf', row_spectra, own_cols, preferred_element_typ...  17.2 us
    dynamic_slice x2, local copies, waits for them, and re-layouts, correlate_one_block(): own_cols = lax.dynamic_slice_in_dim(col_spectra, first_col, block_cols, 0)  17 us
    unnamed x10, local copies, waits for them, and re-layouts  13.4 us
    all_to_all x1, waiting for transfers between devices, local(): lax.all_to_all(outgoing.reshape(row_count, CAP, SEGS * NT), 'row', split_...  13.2 us
    dot_general x2, matrix products, correlate_one_block(): jnp.dot(cross.reshape(row_total * block_cols, 2 * NF), inverse, preferred...  13.1 us
  transfers between devices with their start and end apart: 4, of which 3 were waited for; matrix products, arithmetic and copies ran while one was open for 12% of the time, Pallas kernels for 0%

commit v1 on v0

v1 whole, which is shorter than its diff:
```python
import functools
import math

import jax
import jax.numpy as jnp
import numpy as np
from jax import lax
from jax.experimental import pallas as pl
from jax.experimental.pallas import tpu as pltpu
from jax.sharding import PartitionSpec as P

NF = 2048
NT = 4096
LAGS = 1024
SEGS = 8
CH_DEV = 4
CAP = 2
SMOOTH = 32
EDGE = 128
N1 = 16
N2 = NT // N1
F2 = NF // N1
HALF = LAGS // 2
PAIR = 2 * F2
STEPS = NF // PAIR
TILE = 256
TILES = 2 * HALF // TILE


def forward_tables():
    n2 = np.arange(N2)
    f1 = np.arange(N1)
    f2 = np.arange(F2)
    angle = 2 * np.pi * (np.outer(f1, n2) % NT) / NT
    twiddle = np.stack([np.cos(angle), -np.sin(angle)]).astype(np.float32)
    angle = 2 * np.pi * (np.outer(n2, f2) % N2) / N2
    c, s = np.cos(angle), np.sin(angle)
    second = np.block([[c, -s], [s, c]]).astype(np.float32)
    high = second.astype(jnp.bfloat16)
    low = (second - high.astype(np.float32)).astype(jnp.bfloat16)
    f = f1[:, None] + N1 * f2[None, :]
    distance = np.minimum(f + 0.5, NF - f - 0.5)
    taper = np.sin(0.5 * np.pi * np.minimum(distance / EDGE, 1.0)) ** 2
    turn = np.pi * f / NT
    shape = np.stack([taper, np.cos(turn), -np.sin(turn)]).astype(np.float32)
    return twiddle, high, low, shape


def lag_tables():
    m2 = 2 * np.arange(HALF) + 1
    f1 = np.arange(N1)
    f2 = N1 * np.arange(F2)
    a = np.pi * (np.outer(f1, m2) % (2 * NT)) / NT
    b = np.pi * (np.outer(f2, m2) % (2 * NT)) / NT
    ac, as_, bc, bs = [jnp.asarray(t, jnp.float32) for t in (np.cos(a), np.sin(a), np.cos(b), np.sin(b))]
    c = ac[:, None] * bc[None] - as_[:, None] * bs[None]
    s = -(as_[:, None] * bc[None] + ac[:, None] * bs[None])
    c = c.reshape(STEPS, PAIR, HALF).astype(jnp.bfloat16)
    s = s.reshape(STEPS, PAIR, HALF).astype(jnp.bfloat16)
    parts = [t[:, :, k : k + TILE] for t in (c, s) for k in range(0, HALF, TILE)]
    return jnp.stack(parts, axis=1)


def shifted(value, lanes, amount):
    rolled = pltpu.roll(value, amount % F2, 1)
    source = lanes - amount
    return jnp.where((source >= 0) & (source < F2), rolled, 0.0)


def spectra_kernel(x_ref, tw_ref, hi_ref, lo_ref, shape_ref, row_ref, col_ref, z_ref):
    rows = x_ref.shape[0]
    cosines = np.cos(2 * np.pi * np.arange(N1) / N1)
    sines = np.sin(2 * np.pi * np.arange(N1) / N1)

    def combine(values, weights):
        total = None
        for v, w in zip(values, weights):
            if abs(w) < 1e-9:
                continue
            term = v if abs(w - 1) < 1e-9 else (-v if abs(w + 1) < 1e-9 else v * np.float32(w))
            total = term if total is None else total + term
        return total

    for h in range(0, N2, 128):
        xs = [x_ref[:, k * N2 + h : k * N2 + h + 128].astype(jnp.float32) for k in range(N1)]
        even = [xs[k] + xs[k + N1 // 2] for k in range(N1 // 2)]
        odd = [xs[k] - xs[k + N1 // 2] for k in range(N1 // 2)]
        for f in range(N1 // 2 + 1):
            src = even if f % 2 == 0 else odd
            re = combine(src, [cosines[f * k % N1] for k in range(N1 // 2)])
            im = combine(src, [-sines[f * k % N1] for k in range(N1 // 2)])
            for f1, sign in {f: 1.0, (N1 - f) % N1: -1.0}.items() if f not in (0, N1 // 2) else ((f, 1.0),):
                tc = tw_ref[0, f1 : f1 + 1, h : h + 128]
                ts = tw_ref[1, f1 : f1 + 1, h : h + 128]
                if im is None:
                    zr, zi = re * tc, re * ts
                else:
                    i = im if sign > 0 else -im
                    zr, zi = re * tc - i * ts, re * ts + i * tc
                z_ref[f1 * rows : (f1 + 1) * rows, h : h + 128] = zr
                z_ref[f1 * rows : (f1 + 1) * rows, N2 + h : N2 + h + 128] = zi
    z = z_ref[...]
    zh = z.astype(jnp.bfloat16)
    zl = (z - zh.astype(jnp.float32)).astype(jnp.bfloat16)
    dot = functools.partial(jnp.dot, preferred_element_type=jnp.float32)
    z_ref[:, : 2 * F2] = dot(zh, hi_ref[...]) + dot(zl, hi_ref[...]) + dot(zh, lo_ref[...])

    lanes = lax.broadcasted_iota(jnp.int32, (rows, F2), 1)
    part = lambda f1, c: z_ref[f1 * rows : (f1 + 1) * rows, c * F2 : (c + 1) * F2]
    power = []
    for f1 in range(N1):
        re, im = part(f1, 0), part(f1, 1)
        power.append(re * re + im * im)
    prefix, suffix = [power[0]], [power[-1]]
    for k in range(1, N1):
        prefix.append(prefix[-1] + power[k])
        suffix.append(suffix[-1] + power[N1 - 1 - k])
    suffix = suffix[::-1]
    total = prefix[-1]
    reach = SMOOTH // N1
    middle = total
    for k in range(1, reach):
        middle = middle + shifted(total, lanes, k) + shifted(total, lanes, -k)
    for f1 in range(N1):
        window = middle + shifted(suffix[f1], lanes, reach) + shifted(prefix[f1], lanes, -reach)
        scale = shape_ref[0, f1 : f1 + 1] * lax.rsqrt(window * (1.0 / (2 * SMOOTH + 1)) + 1e-06)
        re, im = part(f1, 0) * scale, part(f1, 1) * scale
        tc, ts = shape_ref[1, f1 : f1 + 1], shape_ref[2, f1 : f1 + 1]
        tr, ti = re * tc - im * ts, re * ts + im * tc
        for ch in range(rows // SEGS):
            own = slice(ch * SEGS, (ch + 1) * SEGS)
            at = slice(f1 * F2, (f1 + 1) * F2)
            col_ref[ch, :, at] = jnp.concatenate([re[own], im[own]], axis=0).astype(jnp.bfloat16)
            row_ref[ch, :, at] = jnp.concatenate([tr[own], ti[own]], axis=0).astype(jnp.bfloat16)


def spectra_of(segment_rows):
    channels = segment_rows.shape[0] // SEGS
    shape = jax.ShapeDtypeStruct((channels, 2 * SEGS, NF), jnp.bfloat16)
    return pl.pallas_call(
        spectra_kernel,
        out_shape=(shape, shape),
        scratch_shapes=[pltpu.VMEM((N1 * channels * SEGS, 2 * N2), jnp.float32)],
        compiler_params=pltpu.CompilerParams(vmem_limit_bytes=48 << 20),
    )(segment_rows, *[jnp.asarray(t) for t in forward_tables()])


def tree(terms):
    while len(terms) > 1:
        terms = [terms[k] + terms[k + 1] for k in range(0, len(terms), 2)]
    return terms[0]


def correlate_kernel(row_total, col_total, a_ref, b_ref, w_ref, keep_ref, flip_ref, out_ref, a32, cross, acc):
    t = pl.program_id(0)
    share = row_total // TILES
    now = lax.rem(t, 2)
    before = 1 - now

    def cross_rows(first):
        for k in range(share):
            g = first + k
            for h in range(0, PAIR, F2):
                lane = slice(h, h + F2)
                real, imag = [], []
                for s in range(SEGS):
                    ar = jnp.broadcast_to(a32[g, s : s + 1, lane], (col_total, F2)).astype(jnp.bfloat16)
                    ai = jnp.broadcast_to(a32[g, SEGS + s : SEGS + s + 1, lane], (col_total, F2)).astype(jnp.bfloat16)
                    br, bi = b_ref[s, :, lane], b_ref[SEGS + s, :, lane]
                    real.append(ar * br + ai * bi)
                    imag.append(ai * br - ar * bi)
                at = pl.ds(pl.multiple_of(g * col_total, 16), col_total)
                cross[now, 0, at, lane] = tree(real)
                cross[now, 1, at, lane] = tree(imag)

    def lag_tile(i):
        part = jnp.dot(cross[before, i // (TILES // 2)], w_ref[0, i], preferred_element_type=jnp.float32)
        acc[i] = acc[i] + part

    def widen():
        a32[...] = a_ref[...].astype(jnp.float32)

    @pl.when(t == 0)
    def _():
        widen()
        acc[...] = jnp.zeros_like(acc)

        @pl.loop(0, TILES)
        def _(i):
            cross_rows(i * share)

    @pl.when((t > 0) & (t < STEPS))
    def _():
        widen()

        @pl.loop(0, TILES)
        def _(i):
            lag_tile(i)
            cross_rows(i * share)

    @pl.when(t == STEPS)
    def _():
        @pl.loop(0, TILES)
        def _(i):
            lag_tile(i)

        keep = keep_ref[...]
        half = TILES // 2
        for k in range(half):
            up = (acc[k] + acc[half + k]) * keep
            down = (acc[k] - acc[half + k]) * keep
            out_ref[:, HALF + k * TILE : HALF + (k + 1) * TILE] = up.astype(jnp.bfloat16)
            turned = jnp.dot(down.astype(jnp.bfloat16), flip_ref[...], preferred_element_type=jnp.float32)
            out_ref[:, HALF - (k + 1) * TILE : HALF - k * TILE] = turned.astype(jnp.bfloat16)


def correlate(row_spectra, col_spectra, keep, tables):
    row_total = row_spectra.shape[0]
    col_total = col_spectra.shape[1]
    pairs = row_total * col_total
    flip = np.eye(TILE, dtype=np.float32)[::-1]
    step = lambda t: jnp.minimum(t, STEPS - 1)
    fixed = lambda shape: pl.BlockSpec(shape, lambda t: (0,) * len(shape), pipeline_mode=pl.Buffered(1))
    return pl.pallas_call(
        functools.partial(correlate_kernel, row_total, col_total),
        grid=(STEPS + 1,),
        in_specs=[
            pl.BlockSpec((row_total, 2 * SEGS, PAIR), lambda t: (0, 0, step(t))),
            pl.BlockSpec((2 * SEGS, col_total, PAIR), lambda t: (0, 0, step(t))),
            pl.BlockSpec((1, TILES, PAIR, TILE), lambda t: (jnp.maximum(t - 1, 0), 0, 0, 0)),
            fixed((pairs, 1)),
            fixed((TILE, TILE)),
        ],
        out_specs=fixed((pairs, LAGS)),
        out_shape=jax.ShapeDtypeStruct((pairs, LAGS), jnp.bfloat16),
        scratch_shapes=[
            pltpu.VMEM((row_total, 2 * SEGS, PAIR), jnp.float32),
            pltpu.VMEM((2, 2, pairs, PAIR), jnp.bfloat16),
            pltpu.VMEM((TILES, pairs, TILE), jnp.float32),
        ],
        compiler_params=pltpu.CompilerParams(vmem_limit_bytes=56 << 20),
    )(row_spectra, col_spectra, tables, keep, jnp.asarray(flip, jnp.bfloat16))


def local(strain, file_channels, file_counts, window_start):
    row_count = lax.axis_size("row")
    col_count = lax.axis_size("col")
    my_row = lax.axis_index("row")
    my_col = lax.axis_index("col")
    slot_total = strain.shape[0]
    window = lax.dynamic_slice_in_dim(strain, window_start[0], SEGS * NT, 1)
    slot_index = jnp.arange(slot_total, dtype=jnp.int32)
    live_slot = slot_index < file_counts[0]
    owner_row = file_channels // CH_DEV // col_count
    local_slot = file_channels % CH_DEV
    same_owner = (owner_row[:, None] == owner_row[None, :]) & live_slot[None, :]
    earlier = slot_index[None, :] < slot_index[:, None]
    position = jnp.sum((same_owner & earlier).astype(jnp.int32), axis=1)
    target = owner_row * CAP + position
    routing = (
        jnp.arange(row_count * CAP, dtype=jnp.int32)[:, None] == target[None, :]
    ) & live_slot[None, :]
    outgoing = jnp.dot(
        routing.astype(jnp.bfloat16), window, preferred_element_type=jnp.float32
    ).astype(jnp.bfloat16)
    labels = jnp.sum(jnp.where(routing, local_slot[None, :] + 1, 0), axis=1) - 1
    tail = jnp.broadcast_to(labels.astype(jnp.bfloat16)[:, None], (row_count * CAP, 128))
    outgoing = jnp.concatenate([outgoing, tail], axis=1)
    arrived = lax.all_to_all(
        outgoing.reshape(row_count, CAP, SEGS * NT + 128), "row", split_axis=0, concat_axis=0, tiled=True
    ).reshape(row_count * CAP, SEGS * NT + 128)
    arrived_labels = arrived[:, SEGS * NT].astype(jnp.float32)
    wanted = jnp.arange(CH_DEV, dtype=jnp.float32)
    picking = (arrived_labels[None, :] == wanted[:, None]).astype(jnp.bfloat16)
    traces = jnp.dot(
        picking, arrived[:, : SEGS * NT], preferred_element_type=jnp.float32
    ).astype(jnp.bfloat16)
    row_own, col_own = spectra_of(traces.reshape(CH_DEV * SEGS, NT))
    col_spectra = lax.all_gather(col_own, "row", axis=0, tiled=True)
    row_spectra = lax.all_gather(row_own, "col", axis=0, tiled=True)
    row_total = row_spectra.shape[0]
    col_total = col_spectra.shape[0]
    col_local = jnp.arange(col_total, dtype=jnp.int32)
    col_ids = (col_local // CH_DEV * col_count + my_col) * CH_DEV + col_local % CH_DEV
    row_ids = my_row * col_count * CH_DEV + jnp.arange(row_total, dtype=jnp.int32)
    norm_scale = 1.0 / math.sqrt(SEGS * NF)
    keep = jnp.where(row_ids[:, None] != col_ids[None, :], norm_scale, 0.0).astype(jnp.float32)
    lagged = correlate(
        row_spectra, jnp.transpose(col_spectra, (1, 0, 2)), keep.reshape(-1, 1), lag_tables()
    )
    return lagged.reshape(row_total, col_total, LAGS)


def solution(mesh):
    placed = (P(("row", "col"), None), P(("row", "col")), P(("row", "col")), P(("row", "col")))
    return jax.shard_map(
        local, mesh=mesh, in_specs=placed, out_specs=P("row", "col", None), check_vma=False
    )
```

time: 390 us -> 112 us (0.29)
  other arithmetic: 193 us -> 5.27 us
  local copies, waits for them, and re-layouts: 83.1 us -> 4.96 us
  matrix products: 54.7 us -> 0.65 us
  blocking collectives: 0 us -> 20.8 us
  waiting for transfers between devices: 27.6 us -> 48 us
  Pallas kernels: 0 us -> 17.4 us
  starting transfers between devices: 9.9 us -> 0.08 us
  loops' own time: 6.55 us -> 0 us
    another operation x14 -> x1, other arithmetic: 181 us -> 2.3 us  [lag_tables(): return jnp.stack(parts, axis=1)]
    dot_general x15 -> x1, matrix products: 54.4 us -> 0.29 us  [local(): jnp.dot(picking, arrived[:, :SEGS * NT], preferred_element_type=jnp.float32)]
    dynamic_slice x18 -> x0, local copies, waits for them, and re-layouts: 42.6 us -> none  [the longest x4 19.6 us: correlate_one_block(): turned = lax.dynamic_slice_in_dim(flipped, first_col, block_cols, 0)]
    all_gather x2, waiting for transfers between devices: 10.4 us -> 47.2 us  [the longest x1 26.2 us: local(): row_spectra = lax.all_gather(row_own, 'col', axis=0, tiled=True)]
    transpose x4 -> x0, local copies, waits for them, and re-layouts: 20.9 us -> none  [the longest x2 10.5 us: correlate_one_block(): jnp.einsum('icsf,jcsf->ijf', row_spectra, turned, preferred_element_type=...]
    all_to_all x0 -> x1, blocking collectives: none -> 20.8 us  [local(): lax.all_to_all(outgoing.reshape(row_count, CAP, SEGS * NT + 128), 'row',...]
    pallas_call x0 -> x2, Pallas kernels: none -> 17.4 us  [the longest x1 15.5 us: correlate(): pl.pallas_call(functools.partial(correlate_kernel, row_total, col_total),...]
    all_to_all x2 -> x0, waiting for transfers between devices: 16.5 us -> none  [the longest x1 13.2 us: local(): lax.all_to_all(outgoing.reshape(row_count, CAP, SEGS * NT), 'row', split_...]
  transfers between devices with their start and end apart: 4 -> 2, of which waited for: 3 -> 2; matrix products, arithmetic and copies ran while one was open for 12% -> 7% of each run, Pallas kernels for 0% -> 0%
where the time goes in v1:
time: 112 us
  waiting for transfers between devices  48 us (43%)
  blocking collectives  20.8 us (19%)
  Pallas kernels  17.4 us (16%)
  between operations  14.9 us (13%)
  other arithmetic  5.27 us (5%)
  local copies, waits for them, and re-layouts  4.96 us (4%)
    all_gather x1, waiting for transfers between devices, local(): row_spectra = lax.all_gather(row_own, 'col', axis=0, tiled=True)  26.2 us
    all_gather x1, waiting for transfers between devices, local(): col_spectra = lax.all_gather(col_own, 'row', axis=0, tiled=True)  21 us
    all_to_all x1, blocking collectives, local(): lax.all_to_all(outgoing.reshape(row_count, CAP, SEGS * NT + 128), 'row',...  20.8 us
    pallas_call x1, Pallas kernels, correlate(): pl.pallas_call(functools.partial(correlate_kernel, row_total, col_total),...  15.5 us
    all_gather x1, local copies, waits for them, and re-layouts, local(): col_spectra = lax.all_gather(col_own, 'row', axis=0, tiled=True)  2.82 us
    another operation x1, other arithmetic, lag_tables(): return jnp.stack(parts, axis=1)  2.3 us
  transfers between devices with their start and end apart: 2, of which 2 were waited for; matrix products, arithmetic and copies ran while one was open for 7% of the time, Pallas kernels for 0%

profile of v1, /device:TPU:0, one launch (start us, length us, event | category | flops | bytes accessed | tf_op | source)
XLA Modules:
  0.0 112.0 jit_solution(11026429327809300556)
XLA Ops:
  6.5 0.0 copy-start
  6.5 0.0 copy-start.3
  6.5 0.0 copy-start.1
  6.5 0.0 copy-start.2
  6.5 0.0 copy-start.4
  6.6 0.0 copy-start.7
  6.6 0.0 copy-start.8
  6.6 0.0 copy-start.5
  6.6 0.0 copy-start.6
  6.6 0.0 all-gather.5.cloned.1.call-start
  6.6 0.8 and_select_fusion.3
  8.1 0.2 convert_reduce_fusion.1
  8.9 0.1 select_reduce_fusion
  9.1 0.0 copy-done
  9.1 0.4 convolution_convert_fusion
  9.4 0.1 broadcast_in_dim.22
  9.5 0.2 reshape.112
  9.8 20.8 %all_to_all.5 = bf16[4,2,32896]{2,1,0:T(2,128)(2,1)S(1)} all-to-all(bf16[4,2,32896]{2,1,0:T(2,128)(2,1)S(1)} %reshape.112), channel_id=1, replica_groups=mesh['row'=4,'col'=8] {'row'}, dimensions={0} | all-to-all | bytes 1052672 | tf_op jit(solution)/shard_map/all_to_all | solution.py:269
  30.5 0.2 reshape.113
  30.7 0.1 convert_reduce_fusion
  30.8 0.3 convolution_convert_fusion.1
  31.1 0.2 reshape.114.x_ref
  31.3 0.0 copy-done.3
  31.3 0.0 copy-done.1
  31.4 0.0 copy-done.2
  31.4 0.0 copy-done.4
  31.4 1.9 %shard_map.127 = (bf16[4,16,2048]{2,1,0:T(8,128)(2,1)}, bf16[4,16,2048]{2,1,0:T(8,128)(2,1)}) custom-call(bf16[32,4096]{1,0:T(8,128)(2,1)S(1)} %reshape.114.x_ref, f32[2,16,256]{2,1,0:T(8,128)S(1)} %copy-done.3, bf16[512,256]{1,0:T(8,128)(2,1)S(1)} %copy-done.1, bf16[512,256]{1,0:T(8,128)(2,1)S(1)} %copy-done.2, f32[3,16,128]{2,1,0:T(8,128)S(1)} %copy-done.4), custom_call_target="tpu_custom_call" | custom-call | tf_op jit(solution)/shard_map/pallas_call | solution.py:140
  33.3 0.0 all-gather.5.cloned.1.call-update
  33.3 0.0 all-gather.3.cloned.1.call-start
  33.3 0.7 all-gather.3.cloned.1.call-update
  34.1 0.1 compare_select_fusion
  34.1 0.9 select_n.64.keep_ref
  35.1 0.0 copy-done.7
  35.1 0.0 copy-done.8
  35.1 0.0 copy-done.5
  35.1 0.0 copy-done.6
  35.1 1.6 %subtract_convert_fusion = (bf16[16,128,512]{2,1,0:T(8,128)(2,1)S(1)}, bf16[16,128,512]{2,1,0:T(8,128)(2,1)S(1)}) fusion(f32[128,512]{1,0:T(8,128)S(1)} %copy-done.6, f32[16,512]{1,0:T(8,128)S(1)} %copy-done.8, f32[128,512]{1,0:T(8,128)S(1)} %copy-done.5, f32[16,512]{1,0:T(8,128)S(1)} %copy-done.7), kind=kLoop, calls=%fused_computation.4 | loop fusion | flops 9437184 | bytes 4784128 | tf_op jit(solution)/shard_map/convert_element_type | solution.py:58
  36.7 0.5 slice_bitcast_fusion.1
  37.2 2.3 %pad_maximum_fusion.w_ref = bf16[8,4,256,256]{3,2,1,0:T(8,128)(2,1)} fusion(bf16[8,1,256,256]{3,2,1,0:T(8,128)(2,1)S(1)} %get-tuple-element.12, bf16[8,1,256,256]{3,2,1,0:T(8,128)(2,1)S(1)} %get-tuple-element.11, bf16[8,1,256,256]{3,2,1,0:T(8,128)(2,1)S(1)} %get-tuple-element.17, bf16[8,1,256,256]{3,2,1,0:T(8,128)(2,1)S(1)} %get-tuple-element.18), kind=kLoop, calls=%fused_computation.2 | loop fusion | flops 6291456 | bytes 8388608 | tf_op jit(solution)/shard_map/stack | solution.py:61
  39.5 21.0 %all-gather.5.cloned.1.call-done = bf16[16,16,2048]{2,1,0:T(8,128)(2,1)} async-done(((bf16[4,16,2048]{2,1,0:T(8,128)(2,1)}), bf16[16,16,2048]{2,1,0:T(8,128)(2,1)}) %all-gather.5.cloned.1.call-update) | async-done | bytes 1048592 | tf_op jit(solution)/shard_map/all_gather | solution.py:279
  60.5 2.8 %copy.35 = bf16[16,16,2048]{2,0,1:T(8,128)(2,1)} copy(bf16[16,16,2048]{2,1,0:T(8,128)(2,1)} %all-gather.5.cloned.1.call-done) | data formatting | bytes 2097152 | tf_op jit(solution)/shard_map/all_gather | solution.py:279
  63.4 26.2 %all-gather.3.cloned.1.call-done.a_ref = bf16[32,16,2048]{2,1,0:T(8,128)(2,1)} async-done(((bf16[4,16,2048]{2,1,0:T(8,128)(2,1)}), bf16[32,16,2048]{2,1,0:T(8,128)(2,1)}) %all-gather.3.cloned.1.call-update) | async-done | bytes 2097168 | tf_op jit(solution)/shard_map/all_gather | solution.py:280
  89.6 15.5 %shard_map.128 = bf16[512,1024]{1,0:T(8,128)(2,1)} custom-call(bf16[32,16,2048]{2,1,0:T(8,128)(2,1)} %all-gather.3.cloned.1.call-done.a_ref, bf16[16,16,2048]{2,1,0:T(8,128)(2,1)} %bitcast.26, bf16[8,4,256,256]{3,2,1,0:T(8,128)(2,1)} %pad_maximum_fusion.w_ref, f32[512,1]{1,0:T(8,128)} %select_n.64.keep_ref, bf16[256,256]{1,0:T(8,128)(2,1)} %constant.108.clone.flip_ref), custom_call_target="tpu_custom_call" | custom-call | tf_op jit(solution)/shard_map/pallas_call | solution.py:224
  (6 shorter events, 0.1 us)
Async XLA Ops:
  6.5 2.5 %copy-start = (bf16[8,33280]{1,0:T(8,128)(2,1)S(1)}, bf16[8,33280]{1,0:T(8,128)(2,1)}, u32[]{:S(2)}) copy-start(bf16[8,33280]{1,0:T(8,128)(2,1)} %param.13) | copy-start | bytes 1597444
  6.5 24.8 %copy-start.3 = (f32[2,16,256]{2,1,0:T(8,128)S(1)}, f32[2,16,256]{2,1,0:T(8,128)}, u32[]{:S(2)}) copy-start(f32[2,16,256]{2,1,0:T(8,128)} %constant.100.clone.tw_ref) | copy-start | bytes 98308
  6.5 24.8 %copy-start.1 = (bf16[512,256]{1,0:T(8,128)(2,1)S(1)}, bf16[512,256]{1,0:T(8,128)(2,1)}, u32[]{:S(2)}) copy-start(bf16[512,256]{1,0:T(8,128)(2,1)} %constant.101.clone.hi_ref) | copy-start | bytes 786436
  6.5 24.8 %copy-start.2 = (bf16[512,256]{1,0:T(8,128)(2,1)S(1)}, bf16[512,256]{1,0:T(8,128)(2,1)}, u32[]{:S(2)}) copy-start(bf16[512,256]{1,0:T(8,128)(2,1)} %constant.102.clone.lo_ref) | copy-start | bytes 786436
  6.5 24.8 %copy-start.4 = (f32[3,16,128]{2,1,0:T(8,128)S(1)}, f32[3,16,128]{2,1,0:T(8,128)}, u32[]{:S(2)}) copy-start(f32[3,16,128]{2,1,0:T(8,128)} %constant.103.clone.shape_ref) | copy-start | bytes 73732
  6.6 28.5 %copy-start.7 = (f32[16,512]{1,0:T(8,128)S(1)}, f32[16,512]{1,0:T(8,128)}, u32[]{:S(2)}) copy-start(f32[16,512]{1,0:T(8,128)} %constant.104.clone) | copy-start | bytes 98308
  6.6 28.5 %copy-start.8 = (f32[16,512]{1,0:T(8,128)S(1)}, f32[16,512]{1,0:T(8,128)}, u32[]{:S(2)}) copy-start(f32[16,512]{1,0:T(8,128)} %constant.105.clone) | copy-start | bytes 98308
  6.6 28.5 %copy-start.5 = (f32[128,512]{1,0:T(8,128)S(1)}, f32[128,512]{1,0:T(8,128)}, u32[]{:S(2)}) copy-start(f32[128,512]{1,0:T(8,128)} %constant.106.clone) | copy-start | bytes 786436
  6.6 28.5 %copy-start.6 = (f32[128,512]{1,0:T(8,128)S(1)}, f32[128,512]{1,0:T(8,128)}, u32[]{:S(2)}) copy-start(f32[128,512]{1,0:T(8,128)} %constant.107.clone) | copy-start | bytes 786436
  6.6 53.9 %all-gather.5.cloned.1.call-start = ((), (), s32[]{:S(2)}) async-start(), calls=%async_computation.2 | async-start | bytes 1310720 | tf_op jit(solution)/shard_map/all_gather | solution.py:279
  33.3 56.3 %all-gather.3.cloned.1.call-start = ((), (), s32[]{:S(2)}) async-start(), calls=%async_computation.1 | async-start | bytes 2359296 | tf_op jit(solution)/shard_map/all_gather | solution.py:280
Sparse Core Ops, SparseCore 0:
  33.4 27.0 all-gather.4
  62.4 27.1 all-gather.2

commit v2 on v1

--- a/solution.py
+++ b/solution.py
@@ -25,6 +25,7 @@
 STEPS = NF // PAIR
 TILE = 256
 TILES = 2 * HALF // TILE
+MESH = pl.DeviceIdType.MESH
 
 
 def forward_tables():
@@ -67,8 +68,51 @@
     return jnp.where((source >= 0) & (source < F2), rolled, 0.0)
 
 
-def spectra_kernel(x_ref, tw_ref, hi_ref, lo_ref, shape_ref, row_ref, col_ref, z_ref):
+def greet(axes):
+    barrier = pltpu.get_barrier_semaphore()
+    count = 0
+    for axis in axes:
+        size, me = lax.axis_size(axis), lax.axis_index(axis)
+        for d in range(1, size):
+            pl.semaphore_signal(barrier, inc=1, device_id={axis: lax.rem(me + d, size)}, device_id_type=MESH)
+            count += 1
+    pl.semaphore_wait(barrier, count)
+
+
+def spectra_kernel(
+    out_ref, tw_ref, hi_ref, lo_ref, shape_ref, row_ref, col_ref, got, x_ref, z_ref, send_sem, recv_sem
+):
+    size, me = lax.axis_size("row"), lax.axis_index("row")
+    greet(("row",))
+
+    def copy_of(d):
+        peer = lax.rem(me + d, size)
+        return pltpu.make_async_remote_copy(
+            src_ref=out_ref.at[peer],
+            dst_ref=got.at[d],
+            send_sem=send_sem.at[d],
+            recv_sem=recv_sem.at[d],
+            device_id={"row": peer},
+            device_id_type=MESH,
+        )
+
+    copies = [copy_of(d) for d in range(1, size)]
+    for copy in copies:
+        copy.start()
+    got[0] = out_ref[me]
+    for copy in copies:
+        copy.wait()
     rows = x_ref.shape[0]
+    slots = [(d, k) for d in range(size) for k in range(CAP)]
+    label = [got[d, k, :, NT:].astype(jnp.float32) for d, k in slots]
+    for ch in range(rows // SEGS):
+        chosen = [v == np.float32(ch) for v in label]
+        for h in range(0, NT, 128):
+            total = None
+            for (d, k), mask in zip(slots, chosen):
+                term = jnp.where(mask, got[d, k, :, h : h + 128].astype(jnp.float32), 0.0)
+                total = term if total is None else total + term
+            x_ref[ch * SEGS : (ch + 1) * SEGS, h : h + 128] = total
     cosines = np.cos(2 * np.pi * np.arange(N1) / N1)
     sines = np.sin(2 * np.pi * np.arange(N1) / N1)
 
@@ -82,7 +126,7 @@
         return total
 
     for h in range(0, N2, 128):
-        xs = [x_ref[:, k * N2 + h : k * N2 + h + 128].astype(jnp.float32) for k in range(N1)]
+        xs = [x_ref[:, k * N2 + h : k * N2 + h + 128] for k in range(N1)]
         even = [xs[k] + xs[k + N1 // 2] for k in range(N1 // 2)]
         odd = [xs[k] - xs[k + N1 // 2] for k in range(N1 // 2)]
         for f in range(N1 // 2 + 1):
@@ -129,20 +173,31 @@
         tr, ti = re * tc - im * ts, re * ts + im * tc
         for ch in range(rows // SEGS):
             own = slice(ch * SEGS, (ch + 1) * SEGS)
-            at = slice(f1 * F2, (f1 + 1) * F2)
-            col_ref[ch, :, at] = jnp.concatenate([re[own], im[own]], axis=0).astype(jnp.bfloat16)
-            row_ref[ch, :, at] = jnp.concatenate([tr[own], ti[own]], axis=0).astype(jnp.bfloat16)
-
-
-def spectra_of(segment_rows):
-    channels = segment_rows.shape[0] // SEGS
-    shape = jax.ShapeDtypeStruct((channels, 2 * SEGS, NF), jnp.bfloat16)
+            t, at = f1 * F2 // PAIR, slice(f1 * F2 % PAIR, f1 * F2 % PAIR + F2)
+            col_ref[t, ch, :, at] = jnp.concatenate([re[own], im[own]], axis=0).astype(jnp.bfloat16)
+            row_ref[t, ch, :, at] = jnp.concatenate([tr[own], ti[own]], axis=0).astype(jnp.bfloat16)
+
+
+def spectra_of(outgoing):
+    size = outgoing.shape[0]
+    rows = CH_DEV * SEGS
+    shape = jax.ShapeDtypeStruct((STEPS, CH_DEV, 2 * SEGS, PAIR), jnp.bfloat16)
     return pl.pallas_call(
         spectra_kernel,
         out_shape=(shape, shape),
-        scratch_shapes=[pltpu.VMEM((N1 * channels * SEGS, 2 * N2), jnp.float32)],
-        compiler_params=pltpu.CompilerParams(vmem_limit_bytes=48 << 20),
-    )(segment_rows, *[jnp.asarray(t) for t in forward_tables()])
+        in_specs=[pl.BlockSpec(memory_space=pltpu.VMEM)] * 5,
+        out_specs=[pl.BlockSpec(memory_space=pltpu.VMEM)] * 2,
+        scratch_shapes=[
+            pltpu.VMEM(outgoing.shape, jnp.bfloat16),
+            pltpu.VMEM((rows, NT), jnp.float32),
+            pltpu.VMEM((N1 * rows, 2 * N2), jnp.float32),
+            pltpu.SemaphoreType.DMA((size,)),
+            pltpu.SemaphoreType.DMA((size,)),
+        ],
+        compiler_params=pltpu.CompilerParams(
+            vmem_limit_bytes=48 << 20, collective_id=0, has_side_effects=True
+        ),
+    )(outgoing, *[jnp.asarray(t) for t in forward_tables()])
 
 
 def tree(terms):
@@ -151,13 +206,55 @@
     return terms[0]
 
 
-def correlate_kernel(row_total, col_total, a_ref, b_ref, w_ref, keep_ref, flip_ref, out_ref, a32, cross, acc):
-    t = pl.program_id(0)
+def correlate_kernel(
+    row_ref, col_ref, w_ref, keep_ref, flip_ref, out_ref, row_all, col_all, a32, b32, b_ref, cross, acc, sems
+):
+    row_total = row_all.shape[1] * CH_DEV
+    col_total = col_all.shape[1] * CH_DEV
     share = row_total // TILES
-    now = lax.rem(t, 2)
-    before = 1 - now
-
-    def cross_rows(first):
+    greet(("row", "col"))
+    plans = []
+    base = 0
+    for axis, own, gathered in (("row", col_ref, col_all), ("col", row_ref, row_all)):
+        size, me = lax.axis_size(axis), lax.axis_index(axis)
+        for d in range(1, size):
+            plans.append((axis, own, gathered, lax.rem(me + d, size), lax.rem(me + size - d, size), me, base + d - 1))
+        base += size - 1
+
+    def copy_of(plan, t, arriving):
+        axis, own, gathered, peer, source, me, k = plan
+        return pltpu.make_async_remote_copy(
+            src_ref=own.at[t],
+            dst_ref=gathered.at[t, source if arriving else me],
+            send_sem=sems.at[0, k, t],
+            recv_sem=sems.at[1, k, t],
+            device_id={axis: peer},
+            device_id_type=MESH,
+        )
+
+    @pl.loop(0, STEPS)
+    def _(t):
+        for plan in plans:
+            copy_of(plan, t, False).start()
+
+    row_me, col_me = lax.axis_index("row"), lax.axis_index("col")
+
+    @pl.loop(0, STEPS)
+    def _(t):
+        col_all[t, row_me] = col_ref[t]
+        row_all[t, col_me] = row_ref[t]
+
+    def arrive(t):
+        for plan in plans:
+            copy_of(plan, t, True).wait_recv()
+        a32[...] = row_all[t].reshape(a32.shape).astype(jnp.float32)
+        for h in range(PAIR // F2):
+            b32[h] = col_all[t, :, :, :, h * F2 : (h + 1) * F2].reshape(b32.shape[1:]).astype(jnp.float32)
+            for k in range(2 * SEGS):
+                rows = b32[h, pl.ds(k, col_total, stride=2 * SEGS), :]
+                b_ref[k, :, h * F2 : (h + 1) * F2] = rows.astype(jnp.bfloat16)
+
+    def cross_rows(first, now):
         for k in range(share):
             g = first + k
             for h in range(0, PAIR, F2):
@@ -173,73 +270,71 @@
                 cross[now, 0, at, lane] = tree(real)
                 cross[now, 1, at, lane] = tree(imag)
 
-    def lag_tile(i):
-        part = jnp.dot(cross[before, i // (TILES // 2)], w_ref[0, i], preferred_element_type=jnp.float32)
+    def lag_tile(i, t):
+        before = lax.rem(t + 1, 2)
+        part = jnp.dot(cross[before, i // (TILES // 2)], w_ref[t - 1, i], preferred_element_type=jnp.float32)
         acc[i] = acc[i] + part
 
-    def widen():
-        a32[...] = a_ref[...].astype(jnp.float32)
-
-    @pl.when(t == 0)
-    def _():
-        widen()
-        acc[...] = jnp.zeros_like(acc)
+    acc[...] = jnp.zeros_like(acc)
+    arrive(0)
+
+    @pl.loop(0, TILES)
+    def _(i):
+        cross_rows(i * share, 0)
+
+    @pl.loop(1, STEPS)
+    def _(t):
+        arrive(t)
 
         @pl.loop(0, TILES)
         def _(i):
-            cross_rows(i * share)
-
-    @pl.when((t > 0) & (t < STEPS))
-    def _():
-        widen()
-
-        @pl.loop(0, TILES)
-        def _(i):
-            lag_tile(i)
-            cross_rows(i * share)
-
-    @pl.when(t == STEPS)
-    def _():
-        @pl.loop(0, TILES)
-        def _(i):
-            lag_tile(i)
-
-        keep = keep_ref[...]
-        half = TILES // 2
-        for k in range(half):
-            up = (acc[k] + acc[half + k]) * keep
-            down = (acc[k] - acc[half + k]) * keep
-            out_ref[:, HALF + k * TILE : HALF + (k + 1) * TILE] = up.astype(jnp.bfloat16)
-            turned = jnp.dot(down.astype(jnp.bfloat16), flip_ref[...], preferred_element_type=jnp.float32)
-            out_ref[:, HALF - (k + 1) * TILE : HALF - k * TILE] = turned.astype(jnp.bfloat16)
-
-
-def correlate(row_spectra, col_spectra, keep, tables):
-    row_total = row_spectra.shape[0]
-    col_total = col_spectra.shape[1]
+            lag_tile(i, t)
+            cross_rows(i * share, lax.rem(t, 2))
+
+    @pl.loop(0, TILES)
+    def _(i):
+        lag_tile(i, STEPS)
+
+    keep = keep_ref[...]
+    half = TILES // 2
+    for k in range(half):
+        up = (acc[k] + acc[half + k]) * keep
+        down = (acc[k] - acc[half + k]) * keep
+        out_ref[:, HALF + k * TILE : HALF + (k + 1) * TILE] = up.astype(jnp.bfloat16)
+        turned = jnp.dot(down.astype(jnp.bfloat16), flip_ref[...], preferred_element_type=jnp.float32)
+        out_ref[:, HALF - (k + 1) * TILE : HALF - k * TILE] = turned.astype(jnp.bfloat16)
+
+    @pl.loop(0, STEPS)
+    def _(t):
+        for plan in plans:
+            copy_of(plan, t, False).wait_send()
+
+
+def correlate(row_own, col_own, keep, tables):
+    row_count, col_count = lax.axis_size("row"), lax.axis_size("col")
+    row_total, col_total = col_count * CH_DEV, row_count * CH_DEV
     pairs = row_total * col_total
     flip = np.eye(TILE, dtype=np.float32)[::-1]
-    step = lambda t: jnp.minimum(t, STEPS - 1)
-    fixed = lambda shape: pl.BlockSpec(shape, lambda t: (0,) * len(shape), pipeline_mode=pl.Buffered(1))
+    own = row_own.shape[1:]
     return pl.pallas_call(
-        functools.partial(correlate_kernel, row_total, col_total),
-        grid=(STEPS + 1,),
-        in_specs=[
-            pl.BlockSpec((row_total, 2 * SEGS, PAIR), lambda t: (0, 0, step(t))),
-            pl.BlockSpec((2 * SEGS, col_total, PAIR), lambda t: (0, 0, step(t))),
-            pl.BlockSpec((1, TILES, PAIR, TILE), lambda t: (jnp.maximum(t - 1, 0), 0, 0, 0)),
-            fixed((pairs, 1)),
-            fixed((TILE, TILE)),
-        ],
-        out_specs=fixed((pairs, LAGS)),
+        correlate_kernel,
+        in_specs=[pl.BlockSpec(memory_space=pltpu.VMEM)] * 5,
+        out_specs=pl.BlockSpec(memory_space=pltpu.VMEM),
         out_shape=jax.ShapeDtypeStruct((pairs, LAGS), jnp.bfloat16),
         scratch_shapes=[
+            pltpu.VMEM((STEPS, col_count) + own, jnp.bfloat16),
+            pltpu.VMEM((STEPS, row_count) + own, jnp.bfloat16),
             pltpu.VMEM((row_total, 2 * SEGS, PAIR), jnp.float32),
+            pltpu.VMEM((PAIR // F2, col_total * 2 * SEGS, F2), jnp.float32),
+            pltpu.VMEM((2 * SEGS, col_total, PAIR), jnp.bfloat16),
             pltpu.VMEM((2, 2, pairs, PAIR), jnp.bfloat16),
             pltpu.VMEM((TILES, pairs, TILE), jnp.float32),
+            pltpu.SemaphoreType.DMA((2, row_count + col_count - 2, STEPS)),
         ],
-        compiler_params=pltpu.CompilerParams(vmem_limit_bytes=56 << 20),
-    )(row_spectra, col_spectra, tables, keep, jnp.asarray(flip, jnp.bfloat16))
+        compiler_params=pltpu.CompilerParams(
+            vmem_limit_bytes=58 << 20, collective_id=1, has_side_effects=True
+        ),
+    )(row_own, col_own, tables, keep, jnp.asarray(flip, jnp.bfloat16))
 
 
 def local(strain, file_channels, file_counts, window_start):
@@ -264,30 +359,19 @@
         routing.astype(jnp.bfloat16), window, preferred_element_type=jnp.float32
     ).astype(jnp.bfloat16)
     labels = jnp.sum(jnp.where(routing, local_slot[None, :] + 1, 0), axis=1) - 1
-    tail = jnp.broadcast_to(labels.astype(jnp.bfloat16)[:, None], (row_count * CAP, 128))
-    outgoing = jnp.concatenate([outgoing, tail], axis=1)
-    arrived = lax.all_to_all(
-        outgoing.reshape(row_count, CAP, SEGS * NT + 128), "row", split_axis=0, concat_axis=0, tiled=True
-    ).reshape(row_count * CAP, SEGS * NT + 128)
-    arrived_labels = arrived[:, SEGS * NT].astype(jnp.float32)
-    wanted = jnp.arange(CH_DEV, dtype=jnp.float32)
-    picking = (arrived_labels[None, :] == wanted[:, None]).astype(jnp.bfloat16)
-    traces = jnp.dot(
-        picking, arrived[:, : SEGS * NT], preferred_element_type=jnp.float32
-    ).astype(jnp.bfloat16)
-    row_own, col_own = spectra_of(traces.reshape(CH_DEV * SEGS, NT))
-    col_spectra = lax.all_gather(col_own, "row", axis=0, tiled=True)
-    row_spectra = lax.all_gather(row_own, "col", axis=0, tiled=True)
-    row_total = row_spectra.shape[0]
-    col_total = col_spectra.shape[0]
+    tail = jnp.broadcast_to(
+        labels.astype(jnp.bfloat16)[:, None, None], (row_count * CAP, SEGS, 128)
+    )
+    outgoing = jnp.concatenate([outgoing.reshape(row_count * CAP, SEGS, NT), tail], axis=2)
+    row_own, col_own = spectra_of(outgoing.reshape(row_count, CAP, SEGS, NT + 128))
+    row_total = CH_DEV * col_count
+    col_total = CH_DEV * row_count
     col_local = jnp.arange(col_total, dtype=jnp.int32)
     col_ids = (col_local // CH_DEV * col_count + my_col) * CH_DEV + col_local % CH_DEV
     row_ids = my_row * col_count * CH_DEV + jnp.arange(row_total, dtype=jnp.int32)
     norm_scale = 1.0 / math.sqrt(SEGS * NF)
     keep = jnp.where(row_ids[:, None] != col_ids[None, :], norm_scale, 0.0).astype(jnp.float32)
-    lagged = correlate(
-        row_spectra, jnp.transpose(col_spectra, (1, 0, 2)), keep.reshape(-1, 1), lag_tables()
-    )
+    lagged = correlate(row_own, col_own, keep.reshape(-1, 1), lag_tables())
     return lagged.reshape(row_total, col_total, LAGS)
 
 

time: 112 us -> 67.6 us (0.60)
  waiting for transfers between devices: 48 us -> 0 us
  Pallas kernels: 17.4 us -> 52.8 us
  blocking collectives: 20.8 us -> 0 us
  between operations: 14.9 us -> 1.47 us
  local copies, waits for them, and re-layouts: 4.96 us -> 7.57 us
    all_gather x2 -> x0, waiting for transfers between devices: 47.2 us -> none  [the longest x1 26.2 us: local(): row_spectra = lax.all_gather(row_own, 'col', axis=0, tiled=True)]
    pallas_call x2, Pallas kernels: 17.4 us -> 52.8 us  [the longest x1 36.6 us: correlate(): pl.pallas_call(correlate_kernel, in_specs=[pl.BlockSpec(memory_space=pltp...]
    all_to_all x1 -> x0, blocking collectives: 20.8 us -> none  [local(): lax.all_to_all(outgoing.reshape(row_count, CAP, SEGS * NT + 128), 'row',...]
    unnamed x18 -> x24, local copies, waits for them, and re-layouts: 0.05 us -> 6.02 us
    all_gather x1 -> x0, local copies, waits for them, and re-layouts: 2.82 us -> none  [local(): col_spectra = lax.all_gather(col_own, 'row', axis=0, tiled=True)]
  transfers between devices with their start and end apart: 2 -> 0, of which waited for: 2 -> 0; matrix products, arithmetic and copies ran while one was open for 7% -> 0% of each run, Pallas kernels for 0% -> 0%
where the time goes in v2:
time: 67.6 us; the launch traced here: 67.3 us
  Pallas kernels  52.8 us (78%)
  local copies, waits for them, and re-layouts  7.57 us (11%)
  other arithmetic  5.08 us (8%)
  between operations  1.47 us (2%)
    pallas_call x1, Pallas kernels, correlate(): pl.pallas_call(correlate_kernel, in_specs=[pl.BlockSpec(memory_space=pltp...  36.6 us
    pallas_call x1, Pallas kernels, spectra_of(): pl.pallas_call(spectra_kernel, out_shape=(shape, shape), in_specs=[pl.Blo...  16.2 us
    unnamed x24, local copies, waits for them, and re-layouts  6.02 us
    another operation x1, other arithmetic, lag_tables(): return jnp.stack(parts, axis=1)  2.23 us
    convert_element_type x1, other arithmetic, lag_tables(): c = c.reshape(STEPS, PAIR, HALF).astype(jnp.bfloat16)  1.64 us

profile of v2, /device:TPU:0, one launch (start us, length us, event | category | flops | bytes accessed | tf_op | source)
XLA Modules:
  0.0 67.3 jit_solution(10158961751583147499)
XLA Ops:
  0.0 0.0 copy-start
  0.0 0.0 copy-start.9
  0.0 0.0 copy-start.10
  0.0 0.0 copy-start.7
  0.0 0.0 copy-start.8
  0.0 0.8 %and_select_fusion.3 = (s32[8]{0:T(128)S(1)}, s32[8]{0:T(128)S(1)}) fusion(s32[8]{0:T(128)} %param.14), kind=kLoop, calls=%fused_computation.22 | loop fusion | flops 280 | bytes 96 | tf_op jit(solution)/shard_map/jit(floor_divide)/jit(_where)/select_n | solution.py:349
  1.4 0.2 convert_reduce_fusion
  2.3 0.0 copy-done
  2.3 0.4 convolution_convert_fusion
  2.7 0.3 copy.22
  3.0 0.1 select_reduce_fusion
  3.1 0.1 convert_element_type.32
  3.2 0.1 broadcast_in_dim.22
  3.3 0.0 copy-start.3
  3.3 0.9 %copy-done.3 = bf16[512,256]{1,0:T(8,128)(2,1)S(1)} copy-done((bf16[512,256]{1,0:T(8,128)(2,1)S(1)}, bf16[512,256]{1,0:T(8,128)(2,1)}, u32[]{:S(2)}) %copy-start.3) | copy-done | bytes 262168
  4.3 0.0 copy-start.4
  4.3 0.9 %copy-done.4 = bf16[512,256]{1,0:T(8,128)(2,1)S(1)} copy-done((bf16[512,256]{1,0:T(8,128)(2,1)S(1)}, bf16[512,256]{1,0:T(8,128)(2,1)}, u32[]{:S(2)}) %copy-start.4) | copy-done | bytes 262168
  5.2 0.0 copy-start.5
  5.2 0.8 %copy-done.5 = f32[2,16,256]{2,1,0:T(8,128)S(1)} copy-done((f32[2,16,256]{2,1,0:T(8,128)S(1)}, f32[2,16,256]{2,1,0:T(8,128)}, u32[]{:S(2)}) %copy-start.5) | copy-done | bytes 32792
  6.0 0.0 copy-start.6
  6.0 0.7 %copy-done.6 = f32[3,16,128]{2,1,0:T(8,128)S(1)} copy-done((f32[3,16,128]{2,1,0:T(8,128)S(1)}, f32[3,16,128]{2,1,0:T(8,128)}, u32[]{:S(2)}) %copy-start.6) | copy-done | bytes 24600
  6.7 16.2 %shard_map.127 = (bf16[8,4,16,256]{3,2,1,0:T(8,128)(2,1)S(1)}, bf16[8,4,16,256]{3,2,1,0:T(8,128)(2,1)S(1)}) custom-call(bf16[4,2,8,4224]{3,2,1,0:T(8,128)(2,1)S(1)} %pad_maximum_fusion.1.out_ref, f32[2,16,256]{2,1,0:T(8,128)S(1)} %copy-done.5, bf16[512,256]{1,0:T(8,128)(2,1)S(1)} %copy-done.3, bf16[512,256]{1,0:T(8,128)(2,1)S(1)} %copy-done.4, ...), custom_call_target="tpu_custom_call" | custom-call | tf_op jit(solution)/shard_map/pallas_call | solution.py:185
  22.9 0.0 copy-start.1
  22.9 0.0 copy-start.2
  22.9 0.0 copy-done.9
  22.9 0.0 copy-done.10
  22.9 0.0 copy-done.7
  23.0 0.0 copy-done.8
  23.0 1.6 %subtract_convert_fusion = (bf16[16,128,512]{2,1,0:T(8,128)(2,1)S(1)}, bf16[16,128,512]{2,1,0:T(8,128)(2,1)S(1)}) fusion(f32[128,512]{1,0:T(8,128)S(1)} %copy-done.8, f32[16,512]{1,0:T(8,128)S(1)} %copy-done.10, f32[128,512]{1,0:T(8,128)S(1)} %copy-done.7, f32[16,512]{1,0:T(8,128)S(1)} %copy-done.9), kind=kLoop, calls=%fused_computation.3 | loop fusion | flops 9437184 | bytes 4784128 | tf_op jit(solution)/shard_map/convert_element_type | solution.py:59
  24.6 0.5 slice_bitcast_fusion.1
  25.1 0.0 copy-done.1
  25.1 0.0 copy-done.2
  25.1 2.2 %pad_maximum_fusion.w_ref = bf16[8,4,256,256]{3,2,1,0:T(8,128)(2,1)} fusion(bf16[8,1,256,256]{3,2,1,0:T(8,128)(2,1)S(1)} %get-tuple-element.12, bf16[8,1,256,256]{3,2,1,0:T(8,128)(2,1)S(1)} %get-tuple-element.11, bf16[8,1,256,256]{3,2,1,0:T(8,128)(2,1)S(1)} %get-tuple-element.17, bf16[8,1,256,256]{3,2,1,0:T(8,128)(2,1)S(1)} %get-tuple-element.18), kind=kLoop, calls=%fused_computation.1 | loop fusion | flops 6291456 | bytes 8388608 | tf_op jit(solution)/shard_map/stack | solution.py:62
  27.4 0.1 compare_select_fusion
  27.5 0.9 %select_n.64.keep_ref = f32[512,1]{1,0:T(8,128)} reshape(f32[32,16]{1,0:T(8,128)S(1)} %compare_select_fusion) | data formatting | bytes 4096 | tf_op jit(solution)/shard_map/jit(_where)/select_n | solution.py:373
  28.3 36.6 %shard_map.128 = bf16[512,1024]{1,0:T(8,128)(2,1)} custom-call(bf16[8,4,16,256]{3,2,1,0:T(8,128)(2,1)} %copy-done.1, bf16[8,4,16,256]{3,2,1,0:T(8,128)(2,1)} %copy-done.2, bf16[8,4,256,256]{3,2,1,0:T(8,128)(2,1)} %pad_maximum_fusion.w_ref, f32[512,1]{1,0:T(8,128)} %select_n.64.keep_ref, bf16[256,256]{1,0:T(8,128)(2,1)} %constant.108.clone.flip_ref), custom_call_target="tpu_custom_call" | custom-call | tf_op jit(solution)/shard_map/pallas_call | solution.py:319
  64.9 2.3 %copy.26 = bf16[32,16,1024]{2,1,0:T(8,128)(2,1)} copy(bf16[32,16,1024]{2,1,0:T(8,128)(2,1)} %bitcast.26) | data formatting | bytes 2097152
  (6 shorter events, 0.1 us)
Async XLA Ops:
  0.0 2.3 %copy-start = (bf16[8,33280]{1,0:T(8,128)(2,1)S(1)}, bf16[8,33280]{1,0:T(8,128)(2,1)}, u32[]{:S(2)}) copy-start(bf16[8,33280]{1,0:T(8,128)(2,1)} %param.13) | copy-start | bytes 1597444
  0.0 22.9 %copy-start.9 = (f32[16,512]{1,0:T(8,128)S(1)}, f32[16,512]{1,0:T(8,128)}, u32[]{:S(2)}) copy-start(f32[16,512]{1,0:T(8,128)} %constant.104.clone) | copy-start | bytes 98308
  0.0 22.9 %copy-start.10 = (f32[16,512]{1,0:T(8,128)S(1)}, f32[16,512]{1,0:T(8,128)}, u32[]{:S(2)}) copy-start(f32[16,512]{1,0:T(8,128)} %constant.105.clone) | copy-start | bytes 98308
  0.0 22.9 %copy-start.7 = (f32[128,512]{1,0:T(8,128)S(1)}, f32[128,512]{1,0:T(8,128)}, u32[]{:S(2)}) copy-start(f32[128,512]{1,0:T(8,128)} %constant.106.clone) | copy-start | bytes 786436
  0.0 22.9 %copy-start.8 = (f32[128,512]{1,0:T(8,128)S(1)}, f32[128,512]{1,0:T(8,128)}, u32[]{:S(2)}) copy-start(f32[128,512]{1,0:T(8,128)} %constant.107.clone) | copy-start | bytes 786436
  3.3 1.0 %copy-start.3 = (bf16[512,256]{1,0:T(8,128)(2,1)S(1)}, bf16[512,256]{1,0:T(8,128)(2,1)}, u32[]{:S(2)}) copy-start(bf16[512,256]{1,0:T(8,128)(2,1)} %constant.101.clone.hi_ref) | copy-start | bytes 786436
  4.3 0.9 %copy-start.4 = (bf16[512,256]{1,0:T(8,128)(2,1)S(1)}, bf16[512,256]{1,0:T(8,128)(2,1)}, u32[]{:S(2)}) copy-start(bf16[512,256]{1,0:T(8,128)(2,1)} %constant.102.clone.lo_ref) | copy-start | bytes 786436
  5.2 0.8 %copy-start.5 = (f32[2,16,256]{2,1,0:T(8,128)S(1)}, f32[2,16,256]{2,1,0:T(8,128)}, u32[]{:S(2)}) copy-start(f32[2,16,256]{2,1,0:T(8,128)} %constant.100.clone.tw_ref) | copy-start | bytes 98308
  6.0 0.7 %copy-start.6 = (f32[3,16,128]{2,1,0:T(8,128)S(1)}, f32[3,16,128]{2,1,0:T(8,128)}, u32[]{:S(2)}) copy-start(f32[3,16,128]{2,1,0:T(8,128)} %constant.103.clone.shape_ref) | copy-start | bytes 73732
  22.9 2.2 %copy-start.1 = (bf16[8,4,16,256]{3,2,1,0:T(8,128)(2,1)}, bf16[8,4,16,256]{3,2,1,0:T(8,128)(2,1)S(1)}, u32[]{:S(2)}) copy-start(bf16[8,4,16,256]{3,2,1,0:T(8,128)(2,1)S(1)} %get-tuple-element.7.row_ref) | copy-start | bytes 786436
  22.9 2.2 %copy-start.2 = (bf16[8,4,16,256]{3,2,1,0:T(8,128)(2,1)}, bf16[8,4,16,256]{3,2,1,0:T(8,128)(2,1)S(1)}, u32[]{:S(2)}) copy-start(bf16[8,4,16,256]{3,2,1,0:T(8,128)(2,1)S(1)} %get-tuple-element.8.col_ref) | copy-start | bytes 786436

commit v3 on v2

--- a/solution.py
+++ b/solution.py
@@ -53,13 +53,9 @@
     f2 = N1 * np.arange(F2)
     a = np.pi * (np.outer(f1, m2) % (2 * NT)) / NT
     b = np.pi * (np.outer(f2, m2) % (2 * NT)) / NT
-    ac, as_, bc, bs = [jnp.asarray(t, jnp.float32) for t in (np.cos(a), np.sin(a), np.cos(b), np.sin(b))]
-    c = ac[:, None] * bc[None] - as_[:, None] * bs[None]
-    s = -(as_[:, None] * bc[None] + ac[:, None] * bs[None])
-    c = c.reshape(STEPS, PAIR, HALF).astype(jnp.bfloat16)
-    s = s.reshape(STEPS, PAIR, HALF).astype(jnp.bfloat16)
-    parts = [t[:, :, k : k + TILE] for t in (c, s) for k in range(0, HALF, TILE)]
-    return jnp.stack(parts, axis=1)
+    first = np.stack([np.cos(a), np.sin(a)]).astype(np.float32)
+    second = np.stack([np.cos(b), np.sin(b)]).astype(np.float32)
+    return first, second
 
 
 def shifted(value, lanes, amount):
@@ -79,9 +75,14 @@
     pl.semaphore_wait(barrier, count)
 
 
-def spectra_kernel(
-    out_ref, tw_ref, hi_ref, lo_ref, shape_ref, row_ref, col_ref, got, x_ref, z_ref, send_sem, recv_sem
-):
+def spectra_kernel(out_ref, *refs):
+    sources, rest = refs[:6], refs[6:]
+    row_ref, col_ref, w_ref = rest[:3]
+    tw_ref, hi_ref, lo_ref, shape_ref, first_ref, second_ref = consts = rest[3:9]
+    got, x_ref, z_ref, send_sem, recv_sem, const_sem = rest[9:]
+    loads = [pltpu.make_async_copy(f, t, const_sem.at[k]) for k, (f, t) in enumerate(zip(sources, consts))]
+    for load in loads[::-1]:
+        load.start()
     size, me = lax.axis_size("row"), lax.axis_index("row")
     greet(("row",))
 
@@ -100,6 +101,16 @@
     for copy in copies:
         copy.start()
     got[0] = out_ref[me]
+    for load in loads:
+        load.wait()
+    for k in range(HALF // TILE):
+        lane = slice(k * TILE, (k + 1) * TILE)
+        bc, bs = second_ref[0, :, lane], second_ref[1, :, lane]
+        for f1 in range(N1):
+            ac, as_ = first_ref[0, f1 : f1 + 1, lane], first_ref[1, f1 : f1 + 1, lane]
+            t, at = f1 * F2 // PAIR, slice(f1 * F2 % PAIR, f1 * F2 % PAIR + F2)
+            w_ref[t, k, at, :] = (ac * bc - as_ * bs).astype(jnp.bfloat16)
+            w_ref[t, HALF // TILE + k, at, :] = (-(as_ * bc + ac * bs)).astype(jnp.bfloat16)
     for copy in copies:
         copy.wait()
     rows = x_ref.shape[0]
@@ -180,24 +191,27 @@
 
 def spectra_of(outgoing):
     size = outgoing.shape[0]
+    consts = [jnp.asarray(t) for t in forward_tables() + lag_tables()]
     rows = CH_DEV * SEGS
     shape = jax.ShapeDtypeStruct((STEPS, CH_DEV, 2 * SEGS, PAIR), jnp.bfloat16)
     return pl.pallas_call(
         spectra_kernel,
-        out_shape=(shape, shape),
-        in_specs=[pl.BlockSpec(memory_space=pltpu.VMEM)] * 5,
-        out_specs=[pl.BlockSpec(memory_space=pltpu.VMEM)] * 2,
-        scratch_shapes=[
+        out_shape=(shape, shape, jax.ShapeDtypeStruct((STEPS, TILES, PAIR, TILE), jnp.bfloat16)),
+        in_specs=[pl.BlockSpec(memory_space=pltpu.VMEM)] + [pl.BlockSpec(memory_space=pl.ANY)] * len(consts),
+        out_specs=[pl.BlockSpec(memory_space=pltpu.VMEM)] * 3,
+        scratch_shapes=[pltpu.VMEM(t.shape, t.dtype) for t in consts]
+        + [
             pltpu.VMEM(outgoing.shape, jnp.bfloat16),
             pltpu.VMEM((rows, NT), jnp.float32),
             pltpu.VMEM((N1 * rows, 2 * N2), jnp.float32),
             pltpu.SemaphoreType.DMA((size,)),
             pltpu.SemaphoreType.DMA((size,)),
+            pltpu.SemaphoreType.DMA((len(consts),)),
         ],
         compiler_params=pltpu.CompilerParams(
             vmem_limit_bytes=48 << 20, collective_id=0, has_side_effects=True
         ),
-    )(outgoing, *[jnp.asarray(t) for t in forward_tables()])
+    )(outgoing, *consts)
 
 
 def tree(terms):
@@ -207,7 +221,7 @@
 
 
 def correlate_kernel(
-    row_ref, col_ref, w_ref, keep_ref, flip_ref, out_ref, row_all, col_all, a32, b32, b_ref, cross, acc, sems
+    row_ref, col_ref, w_ref, flip_ref, out_hbm, row_all, col_all, a32, b32, b_ref, cross, acc, out_ref, sems, out_sem
 ):
     row_total = row_all.shape[1] * CH_DEV
     col_total = col_all.shape[1] * CH_DEV
@@ -295,14 +309,31 @@
     def _(i):
         lag_tile(i, STEPS)
 
-    keep = keep_ref[...]
+    pairs = row_total * col_total
+    place = lax.broadcasted_iota(jnp.int32, (pairs, TILE), 0) - (col_me * col_total + row_me) * CH_DEV
+    same = place == 0
+    for ch in range(1, CH_DEV):
+        same = same | (place == ch * (col_total + 1))
+    keep = jnp.where(same, 0.0, np.float32(1.0 / math.sqrt(SEGS * NF)))
     half = TILES // 2
+    leaving = []
+
+    def leave(first):
+        lane = pl.ds(first, TILE)
+        copy = pltpu.make_async_copy(out_ref.at[:, lane], out_hbm.at[:, lane], out_sem.at[first // TILE])
+        copy.start()
+        leaving.append(copy)
+
     for k in range(half):
         up = (acc[k] + acc[half + k]) * keep
         down = (acc[k] - acc[half + k]) * keep
         out_ref[:, HALF + k * TILE : HALF + (k + 1) * TILE] = up.astype(jnp.bfloat16)
+        leave(HALF + k * TILE)
         turned = jnp.dot(down.astype(jnp.bfloat16), flip_ref[...], preferred_element_type=jnp.float32)
         out_ref[:, HALF - (k + 1) * TILE : HALF - k * TILE] = turned.astype(jnp.bfloat16)
+        leave(HALF - (k + 1) * TILE)
+    for copy in leaving:
+        copy.wait()
 
     @pl.loop(0, STEPS)
     def _(t):
@@ -310,7 +341,7 @@
             copy_of(plan, t, False).wait_send()
 
 
-def correlate(row_own, col_own, keep, tables):
+def correlate(row_own, col_own, tables):
     row_count, col_count = lax.axis_size("row"), lax.axis_size("col")
     row_total, col_total = col_count * CH_DEV, row_count * CH_DEV
     pairs = row_total * col_total
@@ -318,8 +349,8 @@
     own = row_own.shape[1:]
     return pl.pallas_call(
         correlate_kernel,
-        in_specs=[pl.BlockSpec(memory_space=pltpu.VMEM)] * 5,
-        out_specs=pl.BlockSpec(memory_space=pltpu.VMEM),
+        in_specs=[pl.BlockSpec(memory_space=pltpu.VMEM)] * 4,
+        out_specs=pl.BlockSpec(memory_space=pl.ANY),
         out_shape=jax.ShapeDtypeStruct((pairs, LAGS), jnp.bfloat16),
         scratch_shapes=[
             pltpu.VMEM((STEPS, col_count) + own, jnp.bfloat16),
@@ -329,12 +360,14 @@
             pltpu.VMEM((2 * SEGS, col_total, PAIR), jnp.bfloat16),
             pltpu.VMEM((2, 2, pairs, PAIR), jnp.bfloat16),
             pltpu.VMEM((TILES, pairs, TILE), jnp.float32),
+            pltpu.VMEM((pairs, LAGS), jnp.bfloat16),
             pltpu.SemaphoreType.DMA((2, row_count + col_count - 2, STEPS)),
+            pltpu.SemaphoreType.DMA((LAGS // TILE,)),
         ],
         compiler_params=pltpu.CompilerParams(
             vmem_limit_bytes=58 << 20, collective_id=1, has_side_effects=True
         ),
-    )(row_own, col_own, tables, keep, jnp.asarray(flip, jnp.bfloat16))
+    )(row_own, col_own, tables, jnp.asarray(flip, jnp.bfloat16))
 
 
 def local(strain, file_channels, file_counts, window_start):
@@ -363,15 +396,10 @@
         labels.astype(jnp.bfloat16)[:, None, None], (row_count * CAP, SEGS, 128)
     )
     outgoing = jnp.concatenate([outgoing.reshape(row_count * CAP, SEGS, NT), tail], axis=2)
-    row_own, col_own = spectra_of(outgoing.reshape(row_count, CAP, SEGS, NT + 128))
+    row_own, col_own, tables = spectra_of(outgoing.reshape(row_count, CAP, SEGS, NT + 128))
     row_total = CH_DEV * col_count
     col_total = CH_DEV * row_count
-    col_local = jnp.arange(col_total, dtype=jnp.int32)
-    col_ids = (col_local // CH_DEV * col_count + my_col) * CH_DEV + col_local % CH_DEV
-    row_ids = my_row * col_count * CH_DEV + jnp.arange(row_total, dtype=jnp.int32)
-    norm_scale = 1.0 / math.sqrt(SEGS * NF)
-    keep = jnp.where(row_ids[:, None] != col_ids[None, :], norm_scale, 0.0).astype(jnp.float32)
-    lagged = correlate(row_own, col_own, keep.reshape(-1, 1), lag_tables())
+    lagged = correlate(row_own, col_own, tables)
     return lagged.reshape(row_total, col_total, LAGS)
 
 

time: 67.6 us -> 61.6 us (0.911)
  other arithmetic: 5.08 us -> 1.04 us
  local copies, waits for them, and re-layouts: 7.57 us -> 4.96 us
  Pallas kernels: 52.8 us -> 53.6 us
    another operation x1 -> x0, other arithmetic: 2.23 us -> none  [lag_tables(): return jnp.stack(parts, axis=1)]
    convert_element_type x1 -> x0, other arithmetic: 1.64 us -> none  [lag_tables(): c = c.reshape(STEPS, PAIR, HALF).astype(jnp.bfloat16)]
    unnamed x24 -> x20, local copies, waits for them, and re-layouts: 6.02 us -> 4.8 us
    pallas_call x1, Pallas kernels: 16.2 us -> 17.1 us  [spectra_of(): pl.pallas_call(spectra_kernel, out_shape=(shape, shape, jax.ShapeDtypeStr...]
    select_n x1 -> x0, local copies, waits for them, and re-layouts: 0.87 us -> none  [local(): jnp.where(row_ids[:, None] != col_ids[None, :], norm_scale, 0.0)]
where the time goes in v3:
time: 61.6 us; the launch traced here: 61.4 us
  Pallas kernels  53.6 us (87%)
  local copies, waits for them, and re-layouts  4.96 us (8%)
  between operations  1.47 us (2%)
  other arithmetic  1.04 us (2%)
    pallas_call x1, Pallas kernels, correlate(): pl.pallas_call(correlate_kernel, in_specs=[pl.BlockSpec(memory_space=pltp...  36.5 us
    pallas_call x1, Pallas kernels, spectra_of(): pl.pallas_call(spectra_kernel, out_shape=(shape, shape, jax.ShapeDtypeStr...  17.1 us
    unnamed x20, local copies, waits for them, and re-layouts  4.8 us

profile of v3, /device:TPU:0, one launch (start us, length us, event | category | flops | bytes accessed | tf_op | source)
XLA Modules:
  0.0 61.4 jit_solution(16548269028105516161)
XLA Ops:
  0.0 0.0 copy-start
  1.4 0.7 %and_select_fusion.1 = (s32[8]{0:T(128)S(1)}, s32[8]{0:T(128)S(1)}) fusion(s32[8]{0:T(128)} %param.12), kind=kLoop, calls=%fused_computation.12 | loop fusion | flops 280 | bytes 96 | tf_op jit(solution)/shard_map/jit(floor_divide)/jit(_where)/select_n | solution.py:382
  2.0 0.2 convert_reduce_fusion
  2.2 0.1 select_reduce_fusion
  2.4 0.1 convert_element_type.20
  2.5 0.1 broadcast_in_dim.12
  2.5 0.0 copy-done
  2.5 0.4 convolution_convert_fusion
  2.9 0.0 copy-start.1
  2.9 0.0 copy-start.4
  2.9 0.0 copy-start.5
  2.9 0.0 copy-start.6
  3.0 0.0 copy-start.7
  3.0 0.0 copy-start.8
  3.0 0.3 copy.12
  3.3 0.6 %copy-done.1 = f32[2,128,512]{2,1,0:T(8,128)S(1)} copy-done((f32[2,128,512]{2,1,0:T(8,128)S(1)}, f32[2,128,512]{2,1,0:T(8,128)}, u32[]{:S(2)}) %copy-start.1) | copy-done | bytes 524312
  4.0 0.1 copy-done.4
  4.0 0.1 copy-done.5
  4.1 0.0 copy-done.6
  4.1 0.0 copy-done.7
  4.1 0.0 copy-done.8
  4.1 17.1 %shard_map.109 = (bf16[8,4,16,256]{3,2,1,0:T(8,128)(2,1)S(1)}, bf16[8,4,16,256]{3,2,1,0:T(8,128)(2,1)S(1)}, bf16[8,4,256,256]{3,2,1,0:T(8,128)(2,1)}) custom-call(bf16[4,2,8,4224]{3,2,1,0:T(8,128)(2,1)S(1)} %pad_maximum_fusion.out_ref, f32[2,16,256]{2,1,0:T(8,128)S(1)} %copy-done.7, bf16[512,256]{1,0:T(8,128)(2,1)S(1)} %copy-done.5, ...), custom_call_target="tpu_custom_call" | custom-call | tf_op jit(solution)/shard_map/pallas_call | solution.py:197
  21.2 0.0 copy-start.2
  21.2 0.7 %copy-done.2 = bf16[8,4,16,256]{3,2,1,0:T(8,128)(2,1)} copy-done((bf16[8,4,16,256]{3,2,1,0:T(8,128)(2,1)}, bf16[8,4,16,256]{3,2,1,0:T(8,128)(2,1)S(1)}, u32[]{:S(2)}) %copy-start.2) | copy-done | bytes 262168
  21.9 0.0 copy-start.3
  21.9 0.7 %copy-done.3 = bf16[8,4,16,256]{3,2,1,0:T(8,128)(2,1)} copy-done((bf16[8,4,16,256]{3,2,1,0:T(8,128)(2,1)}, bf16[8,4,16,256]{3,2,1,0:T(8,128)(2,1)S(1)}, u32[]{:S(2)}) %copy-start.3) | copy-done | bytes 262168
  22.6 36.5 %shard_map.110 = bf16[512,1024]{1,0:T(8,128)(2,1)} custom-call(bf16[8,4,16,256]{3,2,1,0:T(8,128)(2,1)} %copy-done.2, bf16[8,4,16,256]{3,2,1,0:T(8,128)(2,1)} %copy-done.3, bf16[8,4,256,256]{3,2,1,0:T(8,128)(2,1)} %get-tuple-element.10.w_ref, bf16[256,256]{1,0:T(8,128)(2,1)} %constant.65.clone.flip_ref), custom_call_target="tpu_custom_call" | custom-call | tf_op jit(solution)/shard_map/pallas_call | solution.py:350
  59.1 2.3 %copy.16 = bf16[32,16,1024]{2,1,0:T(8,128)(2,1)} copy(bf16[32,16,1024]{2,1,0:T(8,128)(2,1)} %bitcast.10) | data formatting | bytes 2097152
  (4 shorter events, 0.1 us)
Async XLA Ops:
  0.0 2.5 %copy-start = (bf16[8,33280]{1,0:T(8,128)(2,1)S(1)}, bf16[8,33280]{1,0:T(8,128)(2,1)}, u32[]{:S(2)}) copy-start(bf16[8,33280]{1,0:T(8,128)(2,1)} %param.11) | copy-start | bytes 1597444
  2.9 1.0 %copy-start.1 = (f32[2,128,512]{2,1,0:T(8,128)S(1)}, f32[2,128,512]{2,1,0:T(8,128)}, u32[]{:S(2)}) copy-start(f32[2,128,512]{2,1,0:T(8,128)} %constant.64.clone.refs_5_) | copy-start | bytes 1572868
  2.9 1.1 %copy-start.4 = (bf16[512,256]{1,0:T(8,128)(2,1)S(1)}, bf16[512,256]{1,0:T(8,128)(2,1)}, u32[]{:S(2)}) copy-start(bf16[512,256]{1,0:T(8,128)(2,1)} %constant.61.clone.refs_2_) | copy-start | bytes 786436
  2.9 1.2 %copy-start.5 = (bf16[512,256]{1,0:T(8,128)(2,1)S(1)}, bf16[512,256]{1,0:T(8,128)(2,1)}, u32[]{:S(2)}) copy-start(bf16[512,256]{1,0:T(8,128)(2,1)} %constant.60.clone.refs_1_) | copy-start | bytes 786436
  2.9 1.2 %copy-start.6 = (f32[2,16,512]{2,1,0:T(8,128)S(1)}, f32[2,16,512]{2,1,0:T(8,128)}, u32[]{:S(2)}) copy-start(f32[2,16,512]{2,1,0:T(8,128)} %constant.63.clone.refs_4_) | copy-start | bytes 196612
  3.0 1.1 %copy-start.7 = (f32[2,16,256]{2,1,0:T(8,128)S(1)}, f32[2,16,256]{2,1,0:T(8,128)}, u32[]{:S(2)}) copy-start(f32[2,16,256]{2,1,0:T(8,128)} %constant.59.clone.refs_0_) | copy-start | bytes 98308
  3.0 1.1 %copy-start.8 = (f32[3,16,128]{2,1,0:T(8,128)S(1)}, f32[3,16,128]{2,1,0:T(8,128)}, u32[]{:S(2)}) copy-start(f32[3,16,128]{2,1,0:T(8,128)} %constant.62.clone.refs_3_) | copy-start | bytes 73732
  21.2 0.7 %copy-start.2 = (bf16[8,4,16,256]{3,2,1,0:T(8,128)(2,1)}, bf16[8,4,16,256]{3,2,1,0:T(8,128)(2,1)S(1)}, u32[]{:S(2)}) copy-start(bf16[8,4,16,256]{3,2,1,0:T(8,128)(2,1)S(1)} %get-tuple-element.8.row_ref) | copy-start | bytes 786436
  21.9 0.7 %copy-start.3 = (bf16[8,4,16,256]{3,2,1,0:T(8,128)(2,1)}, bf16[8,4,16,256]{3,2,1,0:T(8,128)(2,1)S(1)}, u32[]{:S(2)}) copy-start(bf16[8,4,16,256]{3,2,1,0:T(8,128)(2,1)S(1)} %get-tuple-element.9.col_ref) | copy-start | bytes 786436

commit v4 on v3

--- a/solution.py
+++ b/solution.py
@@ -25,6 +25,7 @@
 STEPS = NF // PAIR
 TILE = 256
 TILES = 2 * HALF // TILE
+AHEAD = 2
 MESH = pl.DeviceIdType.MESH
 
 
@@ -226,41 +227,100 @@
     row_total = row_all.shape[1] * CH_DEV
     col_total = col_all.shape[1] * CH_DEV
     share = row_total // TILES
+    row_me, col_me = lax.axis_index("row"), lax.axis_index("col")
+    row_size, col_size = lax.axis_size("row"), lax.axis_size("col")
+    partner = col_me + 1 - 2 * lax.rem(col_me, 2)
+    groups = col_size // 2
+    lag = row_size - 2
     greet(("row", "col"))
-    plans = []
-    base = 0
-    for axis, own, gathered in (("row", col_ref, col_all), ("col", row_ref, row_all)):
-        size, me = lax.axis_size(axis), lax.axis_index(axis)
-        for d in range(1, size):
-            plans.append((axis, own, gathered, lax.rem(me + d, size), lax.rem(me + size - d, size), me, base + d - 1))
-        base += size - 1
-
-    def copy_of(plan, t, arriving):
-        axis, own, gathered, peer, source, me, k = plan
+
+    def always(act):
+        act()
+
+    hops = []
+    for step in (1, -1):
+        for d in range(row_size - 1):
+            behind, last = row_me - step * d, row_me - step * (d + 1)
+            inside = lambda r: (r >= 0) & (r < row_size)
+            may_send = inside(behind) & inside(row_me + step)
+            hops.append((pl.when(may_send), pl.when(inside(last)), "row", row_me + step, behind, last, d))
+    for d in range(1, groups):
+        peer, source = lax.rem(col_me + 2 * d, col_size), lax.rem(col_me + col_size - 2 * d, col_size)
+        hops.append((always, always, "col", peer, col_me, source, 0))
+    for d in range(groups):
+        mine, other = [lax.rem(r + col_size - 2 * d, col_size) for r in (col_me, partner)]
+        hops.append((always, always, "col", partner, mine, other, -1 if d else 0))
+
+    def copy_of(k, t, arriving):
+        _, _, axis, peer, slot, source, passed = hops[k]
+        gathered, own = (col_all, col_ref) if axis == "row" else (row_all, row_ref)
+        place = gathered.at[t, source if arriving else slot]
         return pltpu.make_async_remote_copy(
-            src_ref=own.at[t],
-            dst_ref=gathered.at[t, source if arriving else me],
+            src_ref=own.at[t] if passed == 0 and not arriving else place,
+            dst_ref=place,
             send_sem=sems.at[0, k, t],
             recv_sem=sems.at[1, k, t],
             device_id={axis: peer},
             device_id_type=MESH,
         )
 
-    @pl.loop(0, STEPS)
-    def _(t):
-        for plan in plans:
-            copy_of(plan, t, False).start()
-
-    row_me, col_me = lax.axis_index("row"), lax.axis_index("col")
+    def on_send(k, act):
+        hops[k][0](act)
+
+    def on_arrival(k, act):
+        hops[k][1](act)
+
+    own_hops = [k for k, hop in enumerate(hops) if hop[6] == 0]
+
+    def send_own(t):
+        for k in own_hops:
+            on_send(k, lambda k=k: copy_of(k, t, False).start())
+
+    def within(t):
+        return always if isinstance(t, int) else pl.when(t < STEPS)
+
+    def exchange(p):
+        for d in range(row_size - 1):
+            t = p - d
+            if isinstance(t, int) and t < 0:
+                continue
+
+            def serve(d=d, t=t):
+                for side in range(2):
+                    k = side * (row_size - 1) + d
+                    on_arrival(k, lambda k=k: copy_of(k, t, True).wait_recv())
+                    if d + 1 < row_size - 1:
+                        on_send(k + 1, lambda k=k: copy_of(k + 1, t, False).start())
+
+            within(t)(serve)
+        base = 2 * (row_size - 1)
+        t = p - max(lag - 1, 0)
+        if not isinstance(t, int) or t >= 0:
+
+            def serve_col(t=t):
+                for d in range(1, groups):
+                    copy_of(base + d - 1, t, True).wait_recv()
+                    copy_of(base + groups - 1 + d, t, False).start()
+
+            within(t)(serve_col)
+        t = p + AHEAD
+        within(t)(lambda: send_own(t))
+
+    for t in range(AHEAD):
+        send_own(t)
 
     @pl.loop(0, STEPS)
     def _(t):
         col_all[t, row_me] = col_ref[t]
         row_all[t, col_me] = row_ref[t]
 
+    for p in range(lag):
+        exchange(p)
+
     def arrive(t):
-        for plan in plans:
-            copy_of(plan, t, True).wait_recv()
+        exchange(t + lag)
+        for d in range(groups):
+            copy_of(2 * (row_size - 1) + groups - 1 + d, t, True).wait_recv()
         a32[...] = row_all[t].reshape(a32.shape).astype(jnp.float32)
         for h in range(PAIR // F2):
             b32[h] = col_all[t, :, :, :, h * F2 : (h + 1) * F2].reshape(b32.shape[1:]).astype(jnp.float32)
@@ -320,25 +380,29 @@
 
     def leave(first):
         lane = pl.ds(first, TILE)
-        copy = pltpu.make_async_copy(out_ref.at[:, lane], out_hbm.at[:, lane], out_sem.at[first // TILE])
+        copy = pltpu.make_async_copy(out_ref.at[:, :, lane], out_hbm.at[:, :, lane], out_sem.at[first // TILE])
         copy.start()
         leaving.append(copy)
 
     for k in range(half):
         up = (acc[k] + acc[half + k]) * keep
         down = (acc[k] - acc[half + k]) * keep
-        out_ref[:, HALF + k * TILE : HALF + (k + 1) * TILE] = up.astype(jnp.bfloat16)
+        out_ref[:, :, HALF + k * TILE : HALF + (k + 1) * TILE] = (
+            up.reshape(row_total, col_total, TILE).astype(jnp.bfloat16)
+        )
         leave(HALF + k * TILE)
         turned = jnp.dot(down.astype(jnp.bfloat16), flip_ref[...], preferred_element_type=jnp.float32)
-        out_ref[:, HALF - (k + 1) * TILE : HALF - k * TILE] = turned.astype(jnp.bfloat16)
+        out_ref[:, :, HALF - (k + 1) * TILE : HALF - k * TILE] = (
+            turned.reshape(row_total, col_total, TILE).astype(jnp.bfloat16)
+        )
         leave(HALF - (k + 1) * TILE)
     for copy in leaving:
         copy.wait()
 
     @pl.loop(0, STEPS)
     def _(t):
-        for plan in plans:
-            copy_of(plan, t, False).wait_send()
+        for k in range(len(hops)):
+            on_send(k, lambda k=k: copy_of(k, t, False).wait_send())
 
 
 def correlate(row_own, col_own, tables):
@@ -351,7 +415,7 @@
         correlate_kernel,
         in_specs=[pl.BlockSpec(memory_space=pltpu.VMEM)] * 4,
         out_specs=pl.BlockSpec(memory_space=pl.ANY),
-        out_shape=jax.ShapeDtypeStruct((pairs, LAGS), jnp.bfloat16),
+        out_shape=jax.ShapeDtypeStruct((row_total, col_total, LAGS), jnp.bfloat16),
         scratch_shapes=[
             pltpu.VMEM((STEPS, col_count) + own, jnp.bfloat16),
             pltpu.VMEM((STEPS, row_count) + own, jnp.bfloat16),
@@ -360,8 +424,8 @@
             pltpu.VMEM((2 * SEGS, col_total, PAIR), jnp.bfloat16),
             pltpu.VMEM((2, 2, pairs, PAIR), jnp.bfloat16),
             pltpu.VMEM((TILES, pairs, TILE), jnp.float32),
-            pltpu.VMEM((pairs, LAGS), jnp.bfloat16),
-            pltpu.SemaphoreType.DMA((2, row_count + col_count - 2, STEPS)),
+            pltpu.VMEM((row_total, col_total, LAGS), jnp.bfloat16),
+            pltpu.SemaphoreType.DMA((2, 2 * (row_count - 1) + col_count - 1, STEPS)),
             pltpu.SemaphoreType.DMA((LAGS // TILE,)),
         ],
         compiler_params=pltpu.CompilerParams(
@@ -397,10 +461,7 @@
     )
     outgoing = jnp.concatenate([outgoing.reshape(row_count * CAP, SEGS, NT), tail], axis=2)
     row_own, col_own, tables = spectra_of(outgoing.reshape(row_count, CAP, SEGS, NT + 128))
-    row_total = CH_DEV * col_count
-    col_total = CH_DEV * row_count
-    lagged = correlate(row_own, col_own, tables)
-    return lagged.reshape(row_total, col_total, LAGS)
+    return correlate(row_own, col_own, tables)
 
 
 def solution(mesh):

time: 61.6 us -> 63.1 us (1.024)
  Pallas kernels: 53.6 us -> 55.1 us
    pallas_call x1, Pallas kernels: 36.5 us -> 38 us  [correlate(): pl.pallas_call(correlate_kernel, in_specs=[pl.BlockSpec(memory_space=pltp...]
where the time goes in v4:
time: 63.1 us; the launch traced here: 62.9 us
  Pallas kernels  55.1 us (87%)
  local copies, waits for them, and re-layouts  4.96 us (8%)
  between operations  1.47 us (2%)
  other arithmetic  1.04 us (2%)
    pallas_call x1, Pallas kernels, correlate(): pl.pallas_call(correlate_kernel, in_specs=[pl.BlockSpec(memory_space=pltp...  38 us
    pallas_call x1, Pallas kernels, spectra_of(): pl.pallas_call(spectra_kernel, out_shape=(shape, shape, jax.ShapeDtypeStr...  17.1 us
    unnamed x20, local copies, waits for them, and re-layouts  4.8 us

profile of v4, /device:TPU:0, one launch (start us, length us, event | category | flops | bytes accessed | tf_op | source)
XLA Modules:
  0.0 62.9 jit_solution(11372052264063333252)
XLA Ops:
  0.0 0.0 copy-start
  1.4 0.7 %and_select_fusion.1 = (s32[8]{0:T(128)S(1)}, s32[8]{0:T(128)S(1)}) fusion(s32[8]{0:T(128)} %param.12), kind=kLoop, calls=%fused_computation.12 | loop fusion | flops 280 | bytes 96 | tf_op jit(solution)/shard_map/jit(floor_divide)/jit(_where)/select_n | solution.py:446
  2.0 0.2 convert_reduce_fusion
  2.2 0.1 select_reduce_fusion
  2.4 0.1 convert_element_type.20
  2.5 0.1 broadcast_in_dim.12
  2.5 0.0 copy-done
  2.5 0.4 convolution_convert_fusion
  2.9 0.0 copy-start.1
  2.9 0.0 copy-start.4
  2.9 0.0 copy-start.5
  2.9 0.0 copy-start.6
  3.0 0.0 copy-start.7
  3.0 0.0 copy-start.8
  3.0 0.3 copy.12
  3.3 0.6 copy-done.1
  4.0 0.1 copy-done.4
  4.0 0.1 copy-done.5
  4.1 0.0 copy-done.6
  4.1 0.0 copy-done.7
  4.1 0.0 copy-done.8
  4.1 17.1 %shard_map.109 = (bf16[8,4,16,256]{3,2,1,0:T(8,128)(2,1)S(1)}, bf16[8,4,16,256]{3,2,1,0:T(8,128)(2,1)S(1)}, bf16[8,4,256,256]{3,2,1,0:T(8,128)(2,1)}) custom-call(bf16[4,2,8,4224]{3,2,1,0:T(8,128)(2,1)S(1)} %pad_maximum_fusion.out_ref, f32[2,16,256]{2,1,0:T(8,128)S(1)} %copy-done.7, bf16[512,256]{1,0:T(8,128)(2,1)S(1)} %copy-done.5, ...), custom_call_target="tpu_custom_call" | custom-call | tf_op jit(solution)/shard_map/pallas_call | solution.py:198
  21.2 0.0 copy-start.2
  21.2 0.7 %copy-done.2 = bf16[8,4,16,256]{3,2,1,0:T(8,128)(2,1)} copy-done((bf16[8,4,16,256]{3,2,1,0:T(8,128)(2,1)}, bf16[8,4,16,256]{3,2,1,0:T(8,128)(2,1)S(1)}, u32[]{:S(2)}) %copy-start.2) | copy-done | bytes 262168
  21.9 0.0 copy-start.3
  21.9 0.7 %copy-done.3 = bf16[8,4,16,256]{3,2,1,0:T(8,128)(2,1)} copy-done((bf16[8,4,16,256]{3,2,1,0:T(8,128)(2,1)}, bf16[8,4,16,256]{3,2,1,0:T(8,128)(2,1)S(1)}, u32[]{:S(2)}) %copy-start.3) | copy-done | bytes 262168
  22.6 38.0 %shard_map.110 = bf16[32,16,1024]{2,1,0:T(8,128)(2,1)} custom-call(bf16[8,4,16,256]{3,2,1,0:T(8,128)(2,1)} %copy-done.2, bf16[8,4,16,256]{3,2,1,0:T(8,128)(2,1)} %copy-done.3, bf16[8,4,256,256]{3,2,1,0:T(8,128)(2,1)} %get-tuple-element.10.w_ref, bf16[256,256]{1,0:T(8,128)(2,1)} %constant.65.clone.flip_ref), custom_call_target="tpu_custom_call" | custom-call | tf_op jit(solution)/shard_map/pallas_call | solution.py:414
  60.6 2.3 %copy.16 = bf16[32,16,1024]{2,1,0:T(8,128)(2,1)} copy(bf16[32,16,1024]{2,1,0:T(8,128)(2,1)} %shard_map.110) | data formatting | bytes 2097152
  (4 shorter events, 0.1 us)
Async XLA Ops:
  0.0 2.5 %copy-start = (bf16[8,33280]{1,0:T(8,128)(2,1)S(1)}, bf16[8,33280]{1,0:T(8,128)(2,1)}, u32[]{:S(2)}) copy-start(bf16[8,33280]{1,0:T(8,128)(2,1)} %param.11) | copy-start | bytes 1597444
  2.9 1.0 %copy-start.1 = (f32[2,128,512]{2,1,0:T(8,128)S(1)}, f32[2,128,512]{2,1,0:T(8,128)}, u32[]{:S(2)}) copy-start(f32[2,128,512]{2,1,0:T(8,128)} %constant.64.clone.refs_5_) | copy-start | bytes 1572868
  2.9 1.1 %copy-start.4 = (bf16[512,256]{1,0:T(8,128)(2,1)S(1)}, bf16[512,256]{1,0:T(8,128)(2,1)}, u32[]{:S(2)}) copy-start(bf16[512,256]{1,0:T(8,128)(2,1)} %constant.61.clone.refs_2_) | copy-start | bytes 786436
  2.9 1.2 %copy-start.5 = (bf16[512,256]{1,0:T(8,128)(2,1)S(1)}, bf16[512,256]{1,0:T(8,128)(2,1)}, u32[]{:S(2)}) copy-start(bf16[512,256]{1,0:T(8,128)(2,1)} %constant.60.clone.refs_1_) | copy-start | bytes 786436
  2.9 1.2 %copy-start.6 = (f32[2,16,512]{2,1,0:T(8,128)S(1)}, f32[2,16,512]{2,1,0:T(8,128)}, u32[]{:S(2)}) copy-start(f32[2,16,512]{2,1,0:T(8,128)} %constant.63.clone.refs_4_) | copy-start | bytes 196612
  3.0 1.1 %copy-start.7 = (f32[2,16,256]{2,1,0:T(8,128)S(1)}, f32[2,16,256]{2,1,0:T(8,128)}, u32[]{:S(2)}) copy-start(f32[2,16,256]{2,1,0:T(8,128)} %constant.59.clone.refs_0_) | copy-start | bytes 98308
  3.0 1.1 %copy-start.8 = (f32[3,16,128]{2,1,0:T(8,128)S(1)}, f32[3,16,128]{2,1,0:T(8,128)}, u32[]{:S(2)}) copy-start(f32[3,16,128]{2,1,0:T(8,128)} %constant.62.clone.refs_3_) | copy-start | bytes 73732
  21.2 0.7 %copy-start.2 = (bf16[8,4,16,256]{3,2,1,0:T(8,128)(2,1)}, bf16[8,4,16,256]{3,2,1,0:T(8,128)(2,1)S(1)}, u32[]{:S(2)}) copy-start(bf16[8,4,16,256]{3,2,1,0:T(8,128)(2,1)S(1)} %get-tuple-element.8.row_ref) | copy-start | bytes 786436
  21.9 0.7 %copy-start.3 = (bf16[8,4,16,256]{3,2,1,0:T(8,128)(2,1)}, bf16[8,4,16,256]{3,2,1,0:T(8,128)(2,1)S(1)}, u32[]{:S(2)}) copy-start(bf16[8,4,16,256]{3,2,1,0:T(8,128)(2,1)S(1)} %get-tuple-element.9.col_ref) | copy-start | bytes 786436

commit v5 on v3

--- a/solution.py
+++ b/solution.py
@@ -25,6 +25,7 @@
 STEPS = NF // PAIR
 TILE = 256
 TILES = 2 * HALF // TILE
+GROUP = 2
 MESH = pl.DeviceIdType.MESH
 
 
@@ -238,7 +239,7 @@
     def copy_of(plan, t, arriving):
         axis, own, gathered, peer, source, me, k = plan
         return pltpu.make_async_remote_copy(
-            src_ref=own.at[t],
+            src_ref=own.at[pl.ds(t * GROUP, GROUP)],
             dst_ref=gathered.at[t, source if arriving else me],
             send_sem=sems.at[0, k, t],
             recv_sem=sems.at[1, k, t],
@@ -246,7 +247,7 @@
             device_id_type=MESH,
         )
 
-    @pl.loop(0, STEPS)
+    @pl.loop(0, STEPS // GROUP)
     def _(t):
         for plan in plans:
             copy_of(plan, t, False).start()
@@ -255,15 +256,18 @@
 
     @pl.loop(0, STEPS)
     def _(t):
-        col_all[t, row_me] = col_ref[t]
-        row_all[t, col_me] = row_ref[t]
+        col_all[t // GROUP, row_me, lax.rem(t, GROUP)] = col_ref[t]
+        row_all[t // GROUP, col_me, lax.rem(t, GROUP)] = row_ref[t]
 
     def arrive(t):
-        for plan in plans:
-            copy_of(plan, t, True).wait_recv()
-        a32[...] = row_all[t].reshape(a32.shape).astype(jnp.float32)
+        @pl.when(lax.rem(t, GROUP) == 0)
+        def _():
+            for plan in plans:
+                copy_of(plan, t // GROUP, True).wait_recv()
+
+        a32[...] = row_all[t // GROUP, :, lax.rem(t, GROUP)].reshape(a32.shape).astype(jnp.float32)
         for h in range(PAIR // F2):
-            b32[h] = col_all[t, :, :, :, h * F2 : (h + 1) * F2].reshape(b32.shape[1:]).astype(jnp.float32)
+            b32[h] = col_all[t // GROUP, :, lax.rem(t, GROUP), :, :, h * F2 : (h + 1) * F2].reshape(b32.shape[1:]).astype(jnp.float32)
             for k in range(2 * SEGS):
                 rows = b32[h, pl.ds(k, col_total, stride=2 * SEGS), :]
                 b_ref[k, :, h * F2 : (h + 1) * F2] = rows.astype(jnp.bfloat16)
@@ -290,7 +294,7 @@
         acc[i] = acc[i] + part
 
     acc[...] = jnp.zeros_like(acc)
-    arrive(0)
+    arrive(jnp.int32(0))
 
     @pl.loop(0, TILES)
     def _(i):
@@ -335,7 +339,7 @@
     for copy in leaving:
         copy.wait()
 
-    @pl.loop(0, STEPS)
+    @pl.loop(0, STEPS // GROUP)
     def _(t):
         for plan in plans:
             copy_of(plan, t, False).wait_send()
@@ -353,15 +357,15 @@
         out_specs=pl.BlockSpec(memory_space=pl.ANY),
         out_shape=jax.ShapeDtypeStruct((pairs, LAGS), jnp.bfloat16),
         scratch_shapes=[
-            pltpu.VMEM((STEPS, col_count) + own, jnp.bfloat16),
-            pltpu.VMEM((STEPS, row_count) + own, jnp.bfloat16),
+            pltpu.VMEM((STEPS // GROUP, col_count, GROUP) + own, jnp.bfloat16),
+            pltpu.VMEM((STEPS // GROUP, row_count, GROUP) + own, jnp.bfloat16),
             pltpu.VMEM((row_total, 2 * SEGS, PAIR), jnp.float32),
             pltpu.VMEM((PAIR // F2, col_total * 2 * SEGS, F2), jnp.float32),
             pltpu.VMEM((2 * SEGS, col_total, PAIR), jnp.bfloat16),
             pltpu.VMEM((2, 2, pairs, PAIR), jnp.bfloat16),
             pltpu.VMEM((TILES, pairs, TILE), jnp.float32),
             pltpu.VMEM((pairs, LAGS), jnp.bfloat16),
-            pltpu.SemaphoreType.DMA((2, row_count + col_count - 2, STEPS)),
+            pltpu.SemaphoreType.DMA((2, row_count + col_count - 2, STEPS // GROUP)),
             pltpu.SemaphoreType.DMA((LAGS // TILE,)),
         ],
         compiler_params=pltpu.CompilerParams(

time: 61.6 us -> 61.6 us (level)
  no operation moved by 1% of the time
where the time goes in v5:
time: 61.6 us; the launch traced here: 61.4 us
  Pallas kernels  53.6 us (87%)
  local copies, waits for them, and re-layouts  4.96 us (8%)
  between operations  1.47 us (2%)
  other arithmetic  1.04 us (2%)
    pallas_call x1, Pallas kernels, correlate(): pl.pallas_call(correlate_kernel, in_specs=[pl.BlockSpec(memory_space=pltp...  36.5 us
    pallas_call x1, Pallas kernels, spectra_of(): pl.pallas_call(spectra_kernel, out_shape=(shape, shape, jax.ShapeDtypeStr...  17.1 us
    unnamed x20, local copies, waits for them, and re-layouts  4.8 us

profile of v5, /device:TPU:0, one launch (start us, length us, event | category | flops | bytes accessed | tf_op | source)
XLA Modules:
  0.0 61.4 jit_solution(17002364932703996277)
XLA Ops:
  0.0 0.0 copy-start
  1.4 0.7 %and_select_fusion.1 = (s32[8]{0:T(128)S(1)}, s32[8]{0:T(128)S(1)}) fusion(s32[8]{0:T(128)} %param.12), kind=kLoop, calls=%fused_computation.12 | loop fusion | flops 280 | bytes 96 | tf_op jit(solution)/shard_map/jit(floor_divide)/jit(_where)/select_n | solution.py:386
  2.0 0.2 convert_reduce_fusion
  2.2 0.1 select_reduce_fusion
  2.4 0.1 convert_element_type.20
  2.5 0.1 broadcast_in_dim.12
  2.5 0.0 copy-done
  2.5 0.4 convolution_convert_fusion
  2.9 0.0 copy-start.1
  2.9 0.0 copy-start.4
  2.9 0.0 copy-start.5
  2.9 0.0 copy-start.6
  3.0 0.0 copy-start.7
  3.0 0.0 copy-start.8
  3.0 0.3 copy.12
  3.3 0.6 %copy-done.1 = f32[2,128,512]{2,1,0:T(8,128)S(1)} copy-done((f32[2,128,512]{2,1,0:T(8,128)S(1)}, f32[2,128,512]{2,1,0:T(8,128)}, u32[]{:S(2)}) %copy-start.1) | copy-done | bytes 524312
  4.0 0.1 copy-done.4
  4.0 0.1 copy-done.5
  4.1 0.0 copy-done.6
  4.1 0.0 copy-done.7
  4.1 0.0 copy-done.8
  4.1 17.1 %shard_map.109 = (bf16[8,4,16,256]{3,2,1,0:T(8,128)(2,1)S(1)}, bf16[8,4,16,256]{3,2,1,0:T(8,128)(2,1)S(1)}, bf16[8,4,256,256]{3,2,1,0:T(8,128)(2,1)}) custom-call(bf16[4,2,8,4224]{3,2,1,0:T(8,128)(2,1)S(1)} %pad_maximum_fusion.out_ref, f32[2,16,256]{2,1,0:T(8,128)S(1)} %copy-done.7, bf16[512,256]{1,0:T(8,128)(2,1)S(1)} %copy-done.5, ...), custom_call_target="tpu_custom_call" | custom-call | tf_op jit(solution)/shard_map/pallas_call | solution.py:198
  21.2 0.0 copy-start.2
  21.2 0.7 %copy-done.2 = bf16[8,4,16,256]{3,2,1,0:T(8,128)(2,1)} copy-done((bf16[8,4,16,256]{3,2,1,0:T(8,128)(2,1)}, bf16[8,4,16,256]{3,2,1,0:T(8,128)(2,1)S(1)}, u32[]{:S(2)}) %copy-start.2) | copy-done | bytes 262168
  21.9 0.0 copy-start.3
  21.9 0.7 %copy-done.3 = bf16[8,4,16,256]{3,2,1,0:T(8,128)(2,1)} copy-done((bf16[8,4,16,256]{3,2,1,0:T(8,128)(2,1)}, bf16[8,4,16,256]{3,2,1,0:T(8,128)(2,1)S(1)}, u32[]{:S(2)}) %copy-start.3) | copy-done | bytes 262168
  22.6 36.5 %shard_map.110 = bf16[512,1024]{1,0:T(8,128)(2,1)} custom-call(bf16[8,4,16,256]{3,2,1,0:T(8,128)(2,1)} %copy-done.2, bf16[8,4,16,256]{3,2,1,0:T(8,128)(2,1)} %copy-done.3, bf16[8,4,256,256]{3,2,1,0:T(8,128)(2,1)} %get-tuple-element.10.w_ref, bf16[256,256]{1,0:T(8,128)(2,1)} %constant.65.clone.flip_ref), custom_call_target="tpu_custom_call" | custom-call | tf_op jit(solution)/shard_map/pallas_call | solution.py:354
  59.1 2.3 %copy.16 = bf16[32,16,1024]{2,1,0:T(8,128)(2,1)} copy(bf16[32,16,1024]{2,1,0:T(8,128)(2,1)} %bitcast.10) | data formatting | bytes 2097152
  (4 shorter events, 0.1 us)
Async XLA Ops:
  0.0 2.5 %copy-start = (bf16[8,33280]{1,0:T(8,128)(2,1)S(1)}, bf16[8,33280]{1,0:T(8,128)(2,1)}, u32[]{:S(2)}) copy-start(bf16[8,33280]{1,0:T(8,128)(2,1)} %param.11) | copy-start | bytes 1597444
  2.9 1.0 %copy-start.1 = (f32[2,128,512]{2,1,0:T(8,128)S(1)}, f32[2,128,512]{2,1,0:T(8,128)}, u32[]{:S(2)}) copy-start(f32[2,128,512]{2,1,0:T(8,128)} %constant.64.clone.refs_5_) | copy-start | bytes 1572868
  2.9 1.1 %copy-start.4 = (bf16[512,256]{1,0:T(8,128)(2,1)S(1)}, bf16[512,256]{1,0:T(8,128)(2,1)}, u32[]{:S(2)}) copy-start(bf16[512,256]{1,0:T(8,128)(2,1)} %constant.61.clone.refs_2_) | copy-start | bytes 786436
  2.9 1.2 %copy-start.5 = (bf16[512,256]{1,0:T(8,128)(2,1)S(1)}, bf16[512,256]{1,0:T(8,128)(2,1)}, u32[]{:S(2)}) copy-start(bf16[512,256]{1,0:T(8,128)(2,1)} %constant.60.clone.refs_1_) | copy-start | bytes 786436
  2.9 1.2 %copy-start.6 = (f32[2,16,512]{2,1,0:T(8,128)S(1)}, f32[2,16,512]{2,1,0:T(8,128)}, u32[]{:S(2)}) copy-start(f32[2,16,512]{2,1,0:T(8,128)} %constant.63.clone.refs_4_) | copy-start | bytes 196612
  3.0 1.1 %copy-start.7 = (f32[2,16,256]{2,1,0:T(8,128)S(1)}, f32[2,16,256]{2,1,0:T(8,128)}, u32[]{:S(2)}) copy-start(f32[2,16,256]{2,1,0:T(8,128)} %constant.59.clone.refs_0_) | copy-start | bytes 98308
  3.0 1.1 %copy-start.8 = (f32[3,16,128]{2,1,0:T(8,128)S(1)}, f32[3,16,128]{2,1,0:T(8,128)}, u32[]{:S(2)}) copy-start(f32[3,16,128]{2,1,0:T(8,128)} %constant.62.clone.refs_3_) | copy-start | bytes 73732
  21.2 0.7 %copy-start.2 = (bf16[8,4,16,256]{3,2,1,0:T(8,128)(2,1)}, bf16[8,4,16,256]{3,2,1,0:T(8,128)(2,1)S(1)}, u32[]{:S(2)}) copy-start(bf16[8,4,16,256]{3,2,1,0:T(8,128)(2,1)S(1)} %get-tuple-element.8.row_ref) | copy-start | bytes 786436
  21.9 0.7 %copy-start.3 = (bf16[8,4,16,256]{3,2,1,0:T(8,128)(2,1)}, bf16[8,4,16,256]{3,2,1,0:T(8,128)(2,1)S(1)}, u32[]{:S(2)}) copy-start(bf16[8,4,16,256]{3,2,1,0:T(8,128)(2,1)S(1)} %get-tuple-element.9.col_ref) | copy-start | bytes 786436
